TPU v7x, 32 devices: a whole 2x2x4 slice. The times are simulated.
32 devices in a mesh: space: 4 (over x, core), dir: 8 (over z, y).
Axes of the slice: x: 2, y: 2, z: 4, core: 2. Of those that a mesh axis runs over, the one named last changes fastest.
Arguments:
- phonon_heat_density: float32 [128, 40, 8, 4, 256], P('dir', None, 'space'), may hold values from 0.01 to 20, as said below
- directions: float32 [3, 128], replicated, may hold values from -1 to 1, as said below
- quad_weight: float32 [128], replicated, may hold values from 0 to 1, as said below
- mirror: int32 [3, 128], replicated, may hold values from 0 to 127, as said below
- band_courant: float32 [40], replicated, may hold values from 0.3 to 1.9
- relax_rate: float32 [40], replicated, may hold values from 0.05 to 0.95
- mode_heat_magnitude: float32 [40], replicated, may hold values from 0.5 to 2
- mode_pulsation: float32 [40], replicated, may hold values from 0.3 to 2.5
- wall_blocks: int32 [4, 16], P('space'), may hold values from 0 to 15, as said below
- wall_count: int32 [4], P('space'), may hold values from 0 to 16, as said below
- wall_facet: int32 [4, 16, 128], P('space'), may hold values from 0 to 6, as said below
Outputs:
- energy_out: float32 [128, 40, 8, 4, 256], P('dir', None, 'space')
- pseudo_kelvin_field: float32 [8, 4, 256], P('space')
Inputs may be any that keep to these rules, and one draw needn't show every extreme that they name: Unit vectors with no zero component; negating any one component of a direction gives another of the directions. `quad_weight`: Positive, summing to 1, equal for directions that differ only in the signs of components. mirror[a, d] is the direction whose vector is that of d with component a negated. `phonon_heat_density`: Positive. `wall_blocks`: the entries of each row are distinct blocks of the tile; the first wall_count[t] of them are its wall blocks. `wall_count`: tiles t and t + 2 hold at most 16 wall blocks together; some pair holds exactly that, with one of its tiles at 16. `wall_facet`: 0 marks a cell that is no wall, and every cell of slots from wall_count[t] on; f from 1 to 6 names the facet normal along axis (f - 1) // 2, positive for odd f and negative for even f.
All inputs are finite; a program needn't handle non-finite values.
Results may differ from a plain program's by a relative error of at most 0.0003.
Values sent between devices are 32-bit elements; how exact they have to be, the bound alone decides.
A program may use at most 128 MiB of HBM per device.

v0:
```python
import jax
import jax.numpy as jnp
from jax import lax
from jax.sharding import PartitionSpec as P

STEPS = 2
NEWTON = 4
BLOCK = 128
WPAIR = 8


def with_halo(shard, sides, width):
    for axis, dim in sides:
        count, length = (lax.axis_size(axis), shard.shape[dim])
        up = [(i, (i + 1) % count) for i in range(count)]
        down = [(j, i) for i, j in up]
        last = lax.slice_in_dim(shard, length - width, length, axis=dim)
        first = lax.slice_in_dim(shard, 0, width, axis=dim)
        before = lax.ppermute(last, axis, up)
        after = lax.ppermute(first, axis, down)
        shard = jnp.concatenate([before, shard, after], axis=dim)
    return shard


def shifted(shard, axis, by):
    count = lax.axis_size(axis)
    return lax.ppermute(shard, axis, [(i, (i + by) % count) for i in range(count)])


def beam_coeffs(courant):
    abs_speed = jnp.abs(courant)
    centre = 1.0 - 1.5 * abs_speed + 0.5 * abs_speed * abs_speed
    near_weight = 2.0 * abs_speed - abs_speed * abs_speed
    far_weight = 0.5 * abs_speed * abs_speed - 0.5 * abs_speed
    forward = courant > 0
    return (
        centre,
        jnp.where(forward, near_weight, 0.0),
        jnp.where(forward, far_weight, 0.0),
        jnp.where(forward, 0.0, near_weight),
        jnp.where(forward, 0.0, far_weight),
    )


def combine(coeffs, centre_field, back_one, back_two, fore_one, fore_two):
    return (
        coeffs[0] * centre_field
        + coeffs[1] * back_one
        + coeffs[2] * back_two
        + coeffs[3] * fore_one
        + coeffs[4] * fore_two
    )


def roll_sweep(field_in, coeffs, axis_num):
    return combine(
        coeffs,
        field_in,
        jnp.roll(field_in, 1, axis_num),
        jnp.roll(field_in, 2, axis_num),
        jnp.roll(field_in, -1, axis_num),
        jnp.roll(field_in, -2, axis_num),
    )


def root_finder_guess(injection_contribution, collision_speed_factor, mode_pulsation):
    pseudo_kelvin_field = jnp.ones_like(injection_contribution)
    for newton_turn in range(NEWTON):
        dimensionless_pulsation = mode_pulsation[:, None] / pseudo_kelvin_field[None, :]
        heat_surplus = jnp.expm1(dimensionless_pulsation)
        mismatch_error = (
            jnp.sum(collision_speed_factor[:, None] / heat_surplus, axis=0) - injection_contribution
        )
        gradient_guess = (
            jnp.sum(
                collision_speed_factor[:, None]
                * dimensionless_pulsation
                * jnp.exp(dimensionless_pulsation)
                / (heat_surplus * heat_surplus),
                axis=0,
            )
            / pseudo_kelvin_field
        )
        pseudo_kelvin_field = jnp.clip(
            pseudo_kelvin_field - mismatch_error / gradient_guess,
            0.5 * pseudo_kelvin_field,
            2.0 * pseudo_kelvin_field,
        )
    return pseudo_kelvin_field


def transport(phonon_heat_density, own_units, band_courant):

    def coeffs_for(axis_num):
        courant = (own_units[axis_num][:, None] * band_courant[None, :])[:, :, None, None, None]
        return beam_coeffs(courant)

    padded = with_halo(phonon_heat_density, (("space", 2),), 2)
    moved = combine(
        coeffs_for(0),
        padded[:, :, 2:-2],
        padded[:, :, 1:-3],
        padded[:, :, :-4],
        padded[:, :, 3:-1],
        padded[:, :, 4:],
    )
    moved = roll_sweep(moved, coeffs_for(1), 4)
    moved = roll_sweep(moved, coeffs_for(2), 3)
    return moved


def reflect_items(spread, item_facets, directions, mirror):
    result = spread
    for axis_num in range(3):
        mirrored = jnp.take(spread, mirror[axis_num], axis=0)
        component = directions[axis_num][:, None, None]
        chosen = (item_facets == 2 * axis_num + 1)[None] & (component > 0) | (
            item_facets == 2 * axis_num + 2
        )[None] & (component < 0)
        result = jnp.where(chosen, mirrored, result)
    return result


def through_dirs(walls_data, slot_facets, directions, mirror):
    local_dirs, band_count, slot_count, lane_count = walls_data.shape
    item_rows = walls_data.reshape(local_dirs, band_count * slot_count, lane_count)
    spread = lax.all_to_all(item_rows, "dir", split_axis=1, concat_axis=0, tiled=True)
    per_device = spread.shape[1]
    item_ids = lax.axis_index("dir") * per_device + jnp.arange(per_device, dtype=jnp.int32)
    item_facets = jnp.take(slot_facets, item_ids % slot_count, axis=0)
    result = reflect_items(spread, item_facets, directions, mirror)
    returned = lax.all_to_all(result, "dir", split_axis=0, concat_axis=1, tiled=True)
    return returned.reshape(local_dirs, band_count, slot_count, lane_count)


def wall_update(phonon_heat_density, blocks, facets, own_count, slot_ids, directions, mirror):
    local_dirs, band_count = (phonon_heat_density.shape[0], phonon_heat_density.shape[1])
    grid_view = phonon_heat_density.reshape(local_dirs, band_count, -1, BLOCK)
    walls_data = jnp.take(grid_view, blocks, axis=2)
    half_axis = lax.axis_size("space") // 2
    spare_data = walls_data[:, :, WPAIR:]
    spare_facets = facets[WPAIR:].astype(jnp.float32)
    lent_data, lent_facets = shifted((spare_data, spare_facets), "space", half_axis)
    padding = jnp.zeros_like(spare_data)
    pooled = jnp.concatenate([walls_data[:, :, :WPAIR], padding], axis=2)
    pooled = lax.dynamic_update_slice_in_dim(pooled, lent_data, own_count, 2)
    pooled_facets = jnp.concatenate([facets[:WPAIR], jnp.zeros_like(facets[WPAIR:])], axis=0)
    pooled_facets = lax.dynamic_update_slice_in_dim(
        pooled_facets, lent_facets.astype(jnp.int32), own_count, 0
    )
    handled = through_dirs(pooled[:, :, :WPAIR], pooled_facets[:WPAIR], directions, mirror)
    repaid = lax.dynamic_slice_in_dim(
        jnp.concatenate([handled, padding], axis=2), own_count, WPAIR, 2
    )
    returned = shifted(repaid, "space", half_axis)
    result = jnp.concatenate([handled, returned], axis=2)
    result = jnp.where((slot_ids < own_count)[None, None, :, None], result, walls_data)
    grid_view = grid_view.at[:, :, blocks].set(result)
    return grid_view.reshape(phonon_heat_density.shape)


def on_device(
    phonon_heat_density,
    directions,
    quad_weight,
    mirror,
    band_courant,
    relax_rate,
    mode_heat_magnitude,
    mode_pulsation,
    wall_blocks,
    wall_count,
    wall_facet,
):
    local_dirs, band_count = (phonon_heat_density.shape[0], phonon_heat_density.shape[1])
    first_dir = lax.axis_index("dir") * local_dirs
    own_units = lax.dynamic_slice_in_dim(directions, first_dir, local_dirs, 1)
    own_weights = lax.dynamic_slice_in_dim(quad_weight, first_dir, local_dirs, 0)
    mesh_volume_count = (
        phonon_heat_density.shape[2] * phonon_heat_density.shape[3] * phonon_heat_density.shape[4]
    )
    own_count = wall_count[0]
    blocks = wall_blocks[0]
    slot_ids = jnp.arange(blocks.shape[0], dtype=jnp.int32)
    facets = jnp.where(slot_ids[:, None] < own_count, wall_facet[0], 0)
    weights = (own_weights[:, None] * relax_rate[None, :]).reshape(-1)
    collision_speed_factor = relax_rate * mode_heat_magnitude
    pseudo_kelvin_field = jnp.ones((mesh_volume_count,), jnp.float32)
    for step_num in range(STEPS):
        phonon_heat_density = wall_update(
            phonon_heat_density, blocks, facets, own_count, slot_ids, directions, mirror
        )
        phonon_heat_density = transport(phonon_heat_density, own_units, band_courant)
        source_local = jnp.tensordot(
            weights,
            phonon_heat_density.reshape(local_dirs * band_count, mesh_volume_count),
            axes=1,
            precision=lax.Precision.HIGHEST,
        )
        injection_contribution = lax.psum(source_local, "dir")
        pseudo_kelvin_field = root_finder_guess(
            injection_contribution, collision_speed_factor, mode_pulsation
        )
        bose_einstein_heat = mode_heat_magnitude[:, None] / jnp.expm1(
            mode_pulsation[:, None] / pseudo_kelvin_field[None, :]
        )
        phonon_heat_density = phonon_heat_density + relax_rate[None, :, None, None, None] * (
            bose_einstein_heat.reshape((1,) + phonon_heat_density.shape[1:]) - phonon_heat_density
        )
    return (phonon_heat_density, pseudo_kelvin_field.reshape(phonon_heat_density.shape[2:]))


def solution(mesh):
    in_specs = (
        P("dir", None, "space", None, None),
        P(),
        P(),
        P(),
        P(),
        P(),
        P(),
        P(),
        P("space", None),
        P("space"),
        P("space", None, None),
    )
    out_specs = (P("dir", None, "space", None, None), P("space", None, None))
    return jax.shard_map(
        on_device, mesh=mesh, in_specs=in_specs, out_specs=out_specs, check_vma=False
    )
```

profile of v0, /device:TPU:0, one launch (start us, length us, event | category | flops | bytes accessed | tf_op | source)
XLA Modules:
  0.0 1150.6 jit_solution(5225938395750662975)
XLA Ops:
  2.0 7.4 reshape.706
  9.4 6.5 copy.63
  15.8 5.7 gather_fusion.1
  21.6 5.8 broadcast_select_fusion.1
  33.7 56.3 %collective-permute-done.1 = f32[16,40,8,128]{3,1,0,2:T(8,128)} collective-permute-done((f32[16,40,8,128]{3,1,0,2:T(8,128)S(1)}, f32[16,40,8,128]{3,1,0,2:T(8,128)}, u32[]{:S(2)}, u32[]{:S(2)}) %collective-permute-start.1) | collective-permute-done | bytes 2621472 | tf_op jit(solution)/shard_map/ppermute | solution.py:27
  99.9 6.1 all-to-all-start
  110.5 54.1 %all-to-all-done = f32[16,320,128]{2,0,1:T(8,128)S(1)} async-done(((f32[16,320,128]{2,0,1:T(8,128)}), f32[16,320,128]{2,0,1:T(8,128)S(1)}, u32[]{:S(2)}, u32[]{:S(2)}) %all-to-all-start) | async-done | bytes 2621472 | tf_op jit(solution)/shard_map/all_to_all | solution.py:127
  175.6 4.9 fusion.33
  180.5 63.3 %all_to_all.66 = f32[128,40,128]{2,1,0:T(8,128)S(1)} all-to-all(f32[128,40,128]{2,1,0:T(8,128)S(1)} %fusion.33), channel_id=1, replica_groups=mesh['space'=4,'dir'=8] {'dir'}, dimensions={0} | all-to-all | bytes 5242880 | tf_op jit(solution)/shard_map/all_to_all | solution.py:132
  246.5 55.9 %collective-permute-done.2 = f32[16,40,8,128]{3,1,0,2:T(8,128)S(1)} collective-permute-done((f32[16,40,8,128]{3,1,0,2:T(8,128)S(1)}, f32[16,40,8,128]{3,1,0,2:T(8,128)S(1)}, u32[]{:S(2)}, u32[]{:S(2)}) %collective-permute-start.2) | collective-permute-done | bytes 2621472 | tf_op jit(solution)/shard_map/ppermute | solution.py:27
  305.4 9.1 scatter_fusion
  314.5 5.8 copy.64
  320.2 7.7 reshape.709
  330.8 111.1 %collective-permute-done.3 = f32[16,40,2,4,256]{4,3,2,1,0:T(4,128)} collective-permute-done((f32[16,40,2,4,256]{4,3,2,1,0:T(4,128)}, f32[16,40,2,4,256]{4,3,2,1,0:T(4,128)}, u32[]{:S(2)}, u32[]{:S(2)}) %collective-permute-start.3) | collective-permute-done | bytes 5242912 | tf_op jit(solution)/shard_map/ppermute | solution.py:19
  442.6 13.2 %fusion.8 = f32[16,40,2,4,256]{4,3,2,1,0:T(4,128)} fusion(f32[16,40,2,4,256]{4,3,2,1,0:T(4,128)} %collective-permute-done.4, f32[16,40,2,4,256]{4,3,2,1,0:T(4,128)} %reshape.709, f32[16,40,2,4,256]{4,3,2,1,0:T(4,128)} %collective-permute-done.3, f32[16,40]{1,0:T(8,128)S(1)} %get-tuple-element.95, f32[16,40]{1,0:T(8,128)S(1)} %get-tuple-element.97, ...), kind=kLoop, calls=%fused_computation.22 | loop fusion | flops 14417920 | bytes 20984320 | tf_op jit(solution)/shard_map/add | solution.py:47
  455.8 11.8 %fusion.91 = (f32[16,40,2,4,254]{4,3,2,1,0:T(4,128)}, f32[16,40,2,4,254]{4,3,2,1,0:T(4,128)}) fusion(f32[16,40,2,4,256]{4,3,2,1,0:T(4,128)} %fusion.8), kind=kLoop, calls=%fused_computation.212 | loop fusion | bytes 20807680 | tf_op jit(solution)/shard_map/jit(_roll_static)/slice | solution.py:62
  467.6 11.9 %fusion.93 = (f32[16,40,2,4,255]{4,3,2,1,0:T(4,128)}, f32[16,40,2,4,255]{4,3,2,1,0:T(4,128)}) fusion(f32[16,40,2,4,256]{4,3,2,1,0:T(4,128)} %fusion.8), kind=kLoop, calls=%fused_computation.214 | loop fusion | bytes 20889600 | tf_op jit(solution)/shard_map/jit(_roll_static)/slice | solution.py:61
  489.3 29.3 %fusion.16 = f32[16,40,2,4,256]{4,3,2,1,0:T(4,128)} fusion(f32[16,40,2,4,255]{4,3,2,1,0:T(4,128)} %get-tuple-element.57, f32[16,40,2,4,1]{4,3,2,1,0:T(4,128)} %get-tuple-element.59, f32[16,40,2,4,254]{4,3,2,1,0:T(4,128)S(1)} %bitcast.104, f32[16,40,2,4,2]{4,3,2,1,0:T(4,128)S(1)} %get-tuple-element.55, f32[16,40,2,4,1]{4,3,2,1,0:T(4,128)S(1)} %get-tuple-element.58, ...), kind=kLoop, calls=%fused_computation.33 | loop fusion | flops 17039360 | bytes 31470080 | tf_op jit(solution)/shard_map/add | solution.py:47
  518.7 12.1 %fusion.89 = (f32[16,40,2,3,256]{4,3,2,1,0:T(4,128)}, f32[16,40,2,3,256]{4,3,2,1,0:T(4,128)}) fusion(f32[16,40,2,4,256]{4,3,2,1,0:T(4,128)} %fusion.16), kind=kLoop, calls=%fused_computation.210 | loop fusion | bytes 15728640 | tf_op jit(solution)/shard_map/jit(_roll_static)/slice | solution.py:61
  530.8 8.5 fusion.88
  542.1 10.9 fusion.20
  553.1 7.8 reshape.710
  560.8 5.0 fusion.95
  565.9 20.6 %psum.14 = f32[2048]{0:T(1024)S(1)} all-reduce(f32[2048]{0:T(1024)S(1)} %bitcast.114), channel_id=1, replica_groups=mesh['space'=4,'dir'=8] {'dir'}, use_global_device_ids=true, to_apply=%region_2.6 | all-reduce | flops 2048 | bytes 16384 | tf_op jit(solution)/shard_map/psum | solution.py:200
  590.4 6.3 multiply_add_fusion.1
  596.7 7.9 reshape.711
  604.5 6.5 copy.73
  611.0 5.7 gather_fusion.5
  622.1 54.2 %collective-permute-done.5 = f32[16,40,8,128]{3,1,0,2:T(8,128)S(1)} collective-permute-done((f32[16,40,8,128]{3,1,0,2:T(8,128)S(1)}, f32[16,40,8,128]{3,1,0,2:T(8,128)S(1)}, u32[]{:S(2)}, u32[]{:S(2)}) %collective-permute-start.5) | collective-permute-done | bytes 2621472 | tf_op jit(solution)/shard_map/ppermute | solution.py:27
  679.8 58.6 %all_to_all.67 = f32[16,320,128]{2,0,1:T(8,128)S(1)} all-to-all(f32[16,320,128]{2,0,1:T(8,128)S(1)} %copy.67), channel_id=1, replica_groups=mesh['space'=4,'dir'=8] {'dir'}, dimensions={1} | all-to-all | bytes 5242880 | tf_op jit(solution)/shard_map/all_to_all | solution.py:127
  746.3 4.9 fusion.31
  751.2 61.9 %all_to_all.68 = f32[128,40,128]{2,1,0:T(8,128)S(1)} all-to-all(f32[128,40,128]{2,1,0:T(8,128)S(1)} %fusion.31), channel_id=1, replica_groups=mesh['space'=4,'dir'=8] {'dir'}, dimensions={0} | all-to-all | bytes 5242880 | tf_op jit(solution)/shard_map/all_to_all | solution.py:132
  815.6 56.0 %collective-permute-done.6 = f32[16,40,8,128]{3,1,0,2:T(8,128)S(1)} collective-permute-done((f32[16,40,8,128]{3,1,0,2:T(8,128)S(1)}, f32[16,40,8,128]{3,1,0,2:T(8,128)S(1)}, u32[]{:S(2)}, u32[]{:S(2)}) %collective-permute-start.6) | collective-permute-done | bytes 2621472 | tf_op jit(solution)/shard_map/ppermute | solution.py:27
  874.5 9.0 scatter_fusion.1
  883.5 5.7 copy.74
  889.2 7.6 reshape.714
  898.6 112.2 %collective-permute-done.7 = f32[16,40,2,4,256]{4,3,2,1,0:T(4,128)S(1)} collective-permute-done((f32[16,40,2,4,256]{4,3,2,1,0:T(4,128)}, f32[16,40,2,4,256]{4,3,2,1,0:T(4,128)S(1)}, u32[]{:S(2)}, u32[]{:S(2)}) %collective-permute-start.7) | collective-permute-done | bytes 5242912 | tf_op jit(solution)/shard_map/ppermute | solution.py:19
  1011.3 8.6 fusion.2
  1019.9 11.8 %fusion.84 = (f32[16,40,2,4,254]{4,3,2,1,0:T(4,128)}, f32[16,40,2,4,254]{4,3,2,1,0:T(4,128)}) fusion(f32[16,40,2,4,256]{4,3,2,1,0:T(4,128)} %fusion.2), kind=kLoop, calls=%fused_computation.205 | loop fusion | bytes 20807680 | tf_op jit(solution)/shard_map/jit(_roll_static)/slice | solution.py:62
  1031.7 12.0 %fusion.86 = (f32[16,40,2,4,255]{4,3,2,1,0:T(4,128)}, f32[16,40,2,4,255]{4,3,2,1,0:T(4,128)}) fusion(f32[16,40,2,4,256]{4,3,2,1,0:T(4,128)} %fusion.2), kind=kLoop, calls=%fused_computation.207 | loop fusion | bytes 20889600 | tf_op jit(solution)/shard_map/jit(_roll_static)/slice | solution.py:61
  1053.5 18.6 %fusion.25 = f32[16,40,2,4,256]{4,3,2,1,0:T(4,128)} fusion(f32[16,40,2,4,255]{4,3,2,1,0:T(4,128)} %get-tuple-element.43, f32[16,40,2,4,1]{4,3,2,1,0:T(4,128)} %get-tuple-element.45, f32[16,40,2,4,254]{4,3,2,1,0:T(4,128)S(1)} %bitcast.100, f32[16,40,2,4,2]{4,3,2,1,0:T(4,128)S(1)} %get-tuple-element.41, f32[16,40,2,4,1]{4,3,2,1,0:T(4,128)S(1)} %get-tuple-element.44, ...), kind=kLoop, calls=%fused_computation.50 | loop fusion | flops 17039360 | bytes 31470080 | tf_op jit(solution)/shard_map/add | solution.py:47
  1072.1 12.1 %fusion.82 = (f32[16,40,2,3,256]{4,3,2,1,0:T(4,128)}, f32[16,40,2,3,256]{4,3,2,1,0:T(4,128)}) fusion(f32[16,40,2,4,256]{4,3,2,1,0:T(4,128)} %fusion.25), kind=kLoop, calls=%fused_computation.203 | loop fusion | bytes 15728640 | tf_op jit(solution)/shard_map/jit(_roll_static)/slice | solution.py:61
  1084.2 8.5 fusion.81
  1095.5 10.9 fusion.29
  1106.5 8.0 reshape.715
  1114.5 5.0 fusion.96
  1119.5 20.4 %psum.15 = f32[2048]{0:T(1024)S(1)} all-reduce(f32[2048]{0:T(1024)S(1)} %bitcast.113), channel_id=1, replica_groups=mesh['space'=4,'dir'=8] {'dir'}, use_global_device_ids=true, to_apply=%region_11.15 | all-reduce | flops 2048 | bytes 16384 | tf_op jit(solution)/shard_map/psum | solution.py:200
  1143.8 6.3 multiply_add_fusion
  (163 shorter events, 98.5 us)
Async XLA Ops:
  15.8 5.7 copy-start.15
  27.4 2.4 copy-start.4
  30.0 60.0 %collective-permute-start.1 = (f32[16,40,8,128]{3,1,0,2:T(8,128)S(1)}, f32[16,40,8,128]{3,1,0,2:T(8,128)}, u32[]{:S(2)}, u32[]{:S(2)}) collective-permute-start(f32[16,40,8,128]{3,1,0,2:T(8,128)S(1)} %slice.250), channel_id=1, source_target_pairs={{0,16},{8,24},{16,0},{24,8},{1,17},{9,25},{17,1},{25,9},{2,18},{10... | collective-permute-start | bytes 7864328 | tf_op jit(solution)/shard_map/ppermute | solution.py:27
  96.9 9.1 copy-start.13
  96.9 10.8 copy-start.18
  96.9 10.8 copy-start.14
  99.9 64.7 %all-to-all-start = ((f32[16,320,128]{2,0,1:T(8,128)}), f32[16,320,128]{2,0,1:T(8,128)S(1)}, u32[]{:S(2)}, u32[]{:S(2)}) async-start(f32[16,320,128]{2,0,1:T(8,128)} %copy.57), calls=%async_computation | async-start | bytes 5242880 | tf_op jit(solution)/shard_map/all_to_all | solution.py:127
  106.1 3.6 collective-permute-start
  164.6 1.5 copy-start.10
  243.8 58.6 %slice-start = ((s8[5242880]{0:T(1024)(128)(4,1)}), s8[4194304]{0:T(1024)(128)(4,1)S(1)}, s32[]{:S(2)}) async-start(s8[5242880]{0:T(1024)(128)(4,1)} %bitcast.93), calls=%async_computation.4 | async-start | bytes 8388608
  244.1 2.4 copy-start.20
  244.1 58.3 %slice-start.1 = ((s8[5242880]{0:T(1024)(128)(4,1)}), s8[1048576]{0:T(1024)(128)(4,1)S(1)}, s32[]{:S(2)}) async-start(s8[5242880]{0:T(1024)(128)(4,1)} %bitcast.93), calls=%async_computation.5 | async-start | bytes 2097152
  245.0 57.4 %collective-permute-start.2 = (f32[16,40,8,128]{3,1,0,2:T(8,128)S(1)}, f32[16,40,8,128]{3,1,0,2:T(8,128)S(1)}, u32[]{:S(2)}, u32[]{:S(2)}) collective-permute-start(f32[16,40,8,128]{3,1,0,2:T(8,128)S(1)} %pad_dynamic-slice_fusion.1), channel_id=1, source_target_pairs={{0,16},{8,24},{16,0},{24,8},{1,17},{9,25},{17,1},{25,9},{2,18},{10... | collective-permute-start | bytes 7864328 | tf_op jit(solution)/shard_map/ppermute | solution.py:27
  320.2 9.5 copy-start.21
  320.2 9.6 copy-start.12
  320.2 9.8 copy-start.16
  320.2 9.8 copy-start.17
  320.2 10.4 copy-start.19
  327.9 113.9 %collective-permute-start.3 = (f32[16,40,2,4,256]{4,3,2,1,0:T(4,128)}, f32[16,40,2,4,256]{4,3,2,1,0:T(4,128)}, u32[]{:S(2)}, u32[]{:S(2)}) collective-permute-start(f32[16,40,2,4,256]{4,3,2,1,0:T(4,128)} %reshape.709), channel_id=1, source_target_pairs={{0,8},{8,16},{16,24},{24,0},{1,9},{9,17},{17,25},{25,1},{2,10},{10... | collective-permute-start | bytes 15728648 | tf_op jit(solution)/shard_map/ppermute | solution.py:19
  327.9 114.6 %collective-permute-start.4 = (f32[16,40,2,4,256]{4,3,2,1,0:T(4,128)}, f32[16,40,2,4,256]{4,3,2,1,0:T(4,128)}, u32[]{:S(2)}, u32[]{:S(2)}) collective-permute-start(f32[16,40,2,4,256]{4,3,2,1,0:T(4,128)} %reshape.709), channel_id=1, source_target_pairs={{8,0},{16,8},{24,16},{0,24},{9,1},{17,9},{25,17},{1,25},{10,2},{18... | collective-permute-start | bytes 15728648 | tf_op jit(solution)/shard_map/ppermute | solution.py:20
  479.5 4.6 copy-start.1
  479.6 7.9 slice-start.8
  479.6 7.9 slice-start.10
  484.1 3.4 slice-start.9
  484.1 3.4 slice-start.11
  484.2 5.2 copy-start.8
  530.8 8.5 copy-start.3
  539.3 2.8 copy-start.9
  620.2 56.4 %copy-start.5 = (f32[16,40,16,128]{3,1,0,2:T(8,128)}, f32[16,40,16,128]{3,1,0,2:T(8,128)S(1)}, u32[]{:S(2)}) copy-start(f32[16,40,16,128]{3,1,0,2:T(8,128)S(1)} %get-tuple-element.20) | copy-start | bytes 15728644
  620.4 55.9 %collective-permute-start.5 = (f32[16,40,8,128]{3,1,0,2:T(8,128)S(1)}, f32[16,40,8,128]{3,1,0,2:T(8,128)S(1)}, u32[]{:S(2)}, u32[]{:S(2)}) collective-permute-start(f32[16,40,8,128]{3,1,0,2:T(8,128)S(1)} %slice.266), channel_id=1, source_target_pairs={{0,16},{8,24},{16,0},{24,8},{1,17},{9,25},{17,1},{25,9},{2,18},{10... | collective-permute-start | bytes 7864328 | tf_op jit(solution)/shard_map/ppermute | solution.py:27
  813.3 58.3 %slice-start.2 = ((s8[5242880]{0:T(1024)(128)(4,1)}), s8[4194304]{0:T(1024)(128)(4,1)S(1)}, s32[]{:S(2)}) async-start(s8[5242880]{0:T(1024)(128)(4,1)} %bitcast.95), calls=%async_computation.6 | async-start | bytes 8388608
  813.3 58.3 %slice-start.3 = ((s8[5242880]{0:T(1024)(128)(4,1)}), s8[1048576]{0:T(1024)(128)(4,1)S(1)}, s32[]{:S(2)}) async-start(s8[5242880]{0:T(1024)(128)(4,1)} %bitcast.95), calls=%async_computation.7 | async-start | bytes 2097152
  814.2 57.4 %collective-permute-start.6 = (f32[16,40,8,128]{3,1,0,2:T(8,128)S(1)}, f32[16,40,8,128]{3,1,0,2:T(8,128)S(1)}, u32[]{:S(2)}, u32[]{:S(2)}) collective-permute-start(f32[16,40,8,128]{3,1,0,2:T(8,128)S(1)} %pad_dynamic-slice_fusion), channel_id=1, source_target_pairs={{0,16},{8,24},{16,0},{24,8},{1,17},{9,25},{17,1},{25,9},{2,18},{10... | collective-permute-start | bytes 7864328 | tf_op jit(solution)/shard_map/ppermute | solution.py:27
  896.8 114.0 %collective-permute-start.7 = (f32[16,40,2,4,256]{4,3,2,1,0:T(4,128)}, f32[16,40,2,4,256]{4,3,2,1,0:T(4,128)S(1)}, u32[]{:S(2)}, u32[]{:S(2)}) collective-permute-start(f32[16,40,2,4,256]{4,3,2,1,0:T(4,128)} %reshape.714), channel_id=1, source_target_pairs={{0,8},{8,16},{16,24},{24,0},{1,9},{9,17},{17,25},{25,1},{2,10},{10... | collective-permute-start | bytes 15728648 | tf_op jit(solution)/shard_map/ppermute | solution.py:19
  896.8 114.5 %collective-permute-start.8 = (f32[16,40,2,4,256]{4,3,2,1,0:T(4,128)}, f32[16,40,2,4,256]{4,3,2,1,0:T(4,128)S(1)}, u32[]{:S(2)}, u32[]{:S(2)}) collective-permute-start(f32[16,40,2,4,256]{4,3,2,1,0:T(4,128)} %reshape.714), channel_id=1, source_target_pairs={{8,0},{16,8},{24,16},{0,24},{9,1},{17,9},{25,17},{1,25},{10,2},{18... | collective-permute-start | bytes 15728648 | tf_op jit(solution)/shard_map/ppermute | solution.py:20
  1043.7 4.6 copy-start
  1043.7 7.9 slice-start.4
  1043.7 7.9 slice-start.6
  1048.3 3.3 slice-start.5
  1048.3 3.3 slice-start.7
  1048.3 5.2 copy-start.6
  1084.2 8.5 copy-start.2
  1092.7 2.8 copy-start.7
  1143.5 6.6 copy-start.11
where the time goes:
time: 1160 us; the launch traced here: 1150 us
  waiting for transfers between devices  503 us (43%)
  local copies, waits for them, and re-layouts  252 us (22%)
  blocking collectives  225 us (19%)
  other arithmetic  139 us (12%)
  starting transfers between devices  18.7 us (2%)
    ppermute x5, waiting for transfers between devices, shifted(): lax.ppermute(shard, axis, [(i, (i + by) % count) for i in range(count)])  224 us
    ppermute x2, waiting for transfers between devices, with_halo(): before = lax.ppermute(last, axis, up)  223 us
    all_to_all x2, blocking collectives, through_dirs(): lax.all_to_all(result, 'dir', split_axis=0, concat_axis=1, tiled=True)  125 us
    add x6, other arithmetic, combine(): coeffs[0] * centre_field + coeffs[1] * back_one + coeffs[2] * back_two  91.6 us
    slice x8, local copies, waits for them, and re-layouts, roll_sweep(): jnp.roll(field_in, -1, axis_num)  60.3 us
    all_to_all x1, blocking collectives, through_dirs(): lax.all_to_all(item_rows, 'dir', split_axis=1, concat_axis=0, tiled=True)  58.6 us
    all_to_all x1, waiting for transfers between devices, through_dirs(): lax.all_to_all(item_rows, 'dir', split_axis=1, concat_axis=0, tiled=True)  54.1 us
    psum x2, blocking collectives, on_device(): injection_contribution = lax.psum(source_local, 'dir')  41.1 us
  transfers between devices with their start and end apart: 10, of which 10 were waited for; matrix products, arithmetic and copies ran while one was open for 0% of the time, Pallas kernels for 0%

commit v1 on v0

v1 whole, which is shorter than its diff:
```python
import functools

import jax
import jax.numpy as jnp
from jax import lax
from jax.experimental import pallas as pl
from jax.experimental.pallas import tpu as pltpu
from jax.sharding import PartitionSpec as P

STEPS = 2
NEWTON = 4
BLOCK = 128
OCT = 8


def pick(values, index):
    hits = index[:, None] == jnp.arange(values.shape[0], dtype=jnp.int32)[None, :]
    return jnp.sum(jnp.where(hits, values[None, :], jnp.zeros((), values.dtype)), axis=1)


def orbit_order(directions, mirror):
    count = directions.shape[1]
    ids = jnp.arange(count, dtype=jnp.int32)
    positive = (directions > 0).astype(jnp.int32)
    code = positive[0] + 2 * positive[1] + 4 * positive[2]
    rep = ids
    for axis_num in range(3):
        flipped = pick(mirror[axis_num], rep)
        rep = jnp.where(positive[axis_num] > 0, rep, flipped)
    is_rep = code == 7
    rank_of_rep = jnp.sum(
        jnp.where(is_rep[None, :] & (ids[None, :] < rep[:, None]), 1, 0), axis=1
    ).astype(jnp.int32)
    position = rank_of_rep * OCT + code
    order = jnp.sum(
        jnp.where(position[None, :] == ids[:, None], ids[None, :], 0), axis=1
    ).astype(jnp.int32)
    return order, position


def facet_grid(wall_blocks, wall_count, wall_facet, tile_blocks):
    slot_ids = jnp.arange(wall_blocks.shape[0], dtype=jnp.int32)
    hits = (wall_blocks[None, :] == jnp.arange(tile_blocks, dtype=jnp.int32)[:, None]) & (
        slot_ids < wall_count
    )[None, :]
    return jnp.sum(jnp.where(hits[:, :, None], wall_facet[None], 0), axis=1).astype(jnp.int32)


def sweep_kernel(high, tiles, relaxed, coef_ref, facet_ref, e_ref, *rest):
    if relaxed:
        bose_ref, moved_ref, source_ref, now_ref = rest
    else:
        moved_ref, source_ref = rest
        now_ref = e_ref
    band, orbit = pl.program_id(0), pl.program_id(1)
    unit = band * pl.num_programs(1) + orbit
    coef = [coef_ref[unit, i] for i in range(10)]
    rows, width = e_ref.shape[3], e_ref.shape[4]
    row_id = lax.broadcasted_iota(jnp.int32, (rows, width), 0)
    lane_id = lax.broadcasted_iota(jnp.int32, (rows, width), 1)
    height = row_id % high

    @pl.when((band == 0) & (orbit == 0))
    def _():
        source_ref[...] = jnp.zeros_like(source_ref)

    def roll(u, by, axis):
        return pltpu.roll(u, by % u.shape[axis], axis)

    if relaxed:
        for t in range(tiles):
            bose = bose_ref[0, t]
            for o in range(OCT):
                u = e_ref[t, o, 0]
                now_ref[t, o, 0] = u + coef_ref[unit, 10] * (bose - u)

    total = [jnp.zeros((rows, width), jnp.float32) for _ in range(tiles)]
    for o in range(OCT):
        way = [1 if o >> a & 1 else -1 for a in range(3)]
        cells = []
        for t in range(tiles):
            facets = facet_ref[t]
            u = now_ref[t, o, 0]
            for a in range(3):
                facing = 2 * a + 1 if way[a] > 0 else 2 * a + 2
                u = jnp.where(facets == facing, now_ref[t, o ^ (1 << a), 0], u)
            cells.append(u)
        turned = [roll(u, high * way[0], 0) for u in cells]
        for t in range(tiles):
            up = (t - way[0]) % tiles
            edge = row_id < high if way[0] > 0 else row_id >= rows - high
            near = jnp.where(edge, turned[up], turned[t])
            u = coef[0] * cells[t] + coef[1] * near + coef[2] * cells[up]
            u = coef[3] * u + coef[4] * roll(u, way[1], 1) + coef[5] * roll(u, 2 * way[1], 1)
            wrap1 = height < 1 if way[2] > 0 else height >= high - 1
            wrap2 = height < 2 if way[2] > 0 else height >= high - 2
            near = jnp.where(wrap1, roll(u, (1 - high) * way[2], 0), roll(u, way[2], 0))
            far = jnp.where(wrap2, roll(u, (2 - high) * way[2], 0), roll(u, 2 * way[2], 0))
            u = coef[6] * u + coef[7] * near + coef[8] * far
            moved_ref[t, o, 0] = u
            total[t] = total[t] + u
    for t in range(tiles):
        source_ref[t] = source_ref[t] + coef[9] * total[t]


def sweep(high, coefs, facets, field, bose):
    tiles, dirs, bands, rows, width = field.shape
    orbits = dirs // OCT
    block = pl.BlockSpec((tiles, OCT, 1, rows, width), lambda b, o: (0, o, b, 0, 0))
    whole = pl.BlockSpec((tiles, rows, width), lambda b, o: (0, 0, 0))
    in_specs = [pl.BlockSpec(memory_space=pltpu.SMEM), whole, block]
    operands = [coefs, facets, field]
    scratch = []
    if bose is not None:
        in_specs.append(pl.BlockSpec((1, tiles, rows, width), lambda b, o: (b, 0, 0, 0)))
        operands.append(bose)
        scratch.append(pltpu.VMEM((tiles, OCT, 1, rows, width), jnp.float32))
    return pl.pallas_call(
        functools.partial(sweep_kernel, high, tiles, bose is not None),
        grid=(bands, orbits),
        in_specs=in_specs,
        out_specs=[block, whole],
        out_shape=[
            jax.ShapeDtypeStruct(field.shape, jnp.float32),
            jax.ShapeDtypeStruct((tiles, rows, width), jnp.float32),
        ],
        scratch_shapes=scratch,
        compiler_params=pltpu.CompilerParams(dimension_semantics=("arbitrary", "arbitrary")),
    )(*operands)


def beam_coeffs(abs_speed):
    return (
        1.0 - 1.5 * abs_speed + 0.5 * abs_speed * abs_speed,
        2.0 * abs_speed - abs_speed * abs_speed,
        0.5 * abs_speed * abs_speed - 0.5 * abs_speed,
    )


def root_finder_guess(injection_contribution, collision_speed_factor, mode_pulsation):
    pseudo_kelvin_field = jnp.ones_like(injection_contribution)
    for newton_turn in range(NEWTON):
        dimensionless_pulsation = mode_pulsation[:, None] / pseudo_kelvin_field[None, :]
        heat_surplus = jnp.expm1(dimensionless_pulsation)
        mismatch_error = (
            jnp.sum(collision_speed_factor[:, None] / heat_surplus, axis=0) - injection_contribution
        )
        gradient_guess = (
            jnp.sum(
                collision_speed_factor[:, None]
                * dimensionless_pulsation
                * jnp.exp(dimensionless_pulsation)
                / (heat_surplus * heat_surplus),
                axis=0,
            )
            / pseudo_kelvin_field
        )
        pseudo_kelvin_field = jnp.clip(
            pseudo_kelvin_field - mismatch_error / gradient_guess,
            0.5 * pseudo_kelvin_field,
            2.0 * pseudo_kelvin_field,
        )
    return pseudo_kelvin_field


def on_device(
    phonon_heat_density,
    directions,
    quad_weight,
    mirror,
    band_courant,
    relax_rate,
    mode_heat_magnitude,
    mode_pulsation,
    wall_blocks,
    wall_count,
    wall_facet,
):
    local_dirs, bands, wide, high, deep = phonon_heat_density.shape
    tiles, groups = lax.axis_size("space"), lax.axis_size("dir")
    tile, group = lax.axis_index("space"), lax.axis_index("dir")
    rows = wide * high
    share = -(-bands // groups)
    extra = share * groups - bands
    dirs = directions.shape[1]
    orbits = dirs // OCT
    part = dirs // tiles
    part_orbits = orbits // tiles

    order, position = orbit_order(directions, mirror)
    own_facets = facet_grid(
        wall_blocks[0], wall_count[0], wall_facet[0], wide * high * deep // BLOCK
    ).astype(jnp.float32)
    facets = lax.all_gather(own_facets.reshape(rows, deep), "space").astype(jnp.int32)

    def own_bands(values):
        return lax.dynamic_slice_in_dim(jnp.pad(values, (0, extra)), group * share, share)

    courant, rates = own_bands(band_courant), own_bands(relax_rate)
    magnitudes = own_bands(mode_heat_magnitude)
    pulsations = lax.dynamic_slice_in_dim(
        jnp.pad(mode_pulsation, (0, extra), constant_values=1.0), group * share, share
    )
    reps = lax.dynamic_slice_in_dim(
        order.reshape(orbits, OCT)[:, OCT - 1], tile * part_orbits, part_orbits
    )
    columns = []
    for axis_num in range(3):
        unit = jnp.abs(pick(directions[axis_num], reps))
        columns.extend(beam_coeffs(courant[:, None] * unit[None, :]))
    columns.append(rates[:, None] * pick(quad_weight, reps)[None, :])
    columns.append(jnp.broadcast_to(rates[:, None], columns[0].shape))
    coefs = jnp.stack(columns, axis=-1).reshape(share * part_orbits, len(columns))

    field = phonon_heat_density.reshape(local_dirs, bands, rows, deep)
    field = jnp.pad(field, ((0, 0), (0, extra), (0, 0), (0, 0)))
    field = lax.all_to_all(field, "dir", split_axis=1, concat_axis=0, tiled=True)
    field = jnp.take(field, order, axis=0, mode="clip")
    field = lax.all_to_all(field, "space", split_axis=0, concat_axis=0, tiled=True)
    field = field.reshape(tiles, part, share, rows, deep)

    collision_speed_factor = relax_rate * mode_heat_magnitude
    bose = None
    for step_num in range(STEPS):
        field, source = sweep(high, coefs, facets, field, bose)
        source = lax.psum(source, ("space", "dir"))
        if step_num < STEPS - 1:
            kelvin = root_finder_guess(
                source.reshape(-1), collision_speed_factor, mode_pulsation
            ).reshape(source.shape)
            bose = magnitudes[:, None, None, None] / jnp.expm1(
                pulsations[:, None, None, None] / kelvin[None]
            )
    own_source = lax.dynamic_index_in_dim(source, tile, 0, keepdims=False)
    kelvin = root_finder_guess(own_source.reshape(-1), collision_speed_factor, mode_pulsation)
    kelvin = kelvin.reshape(wide, high, deep)
    field = field.reshape(dirs, share, rows, deep)
    field = lax.all_to_all(field, "space", split_axis=0, concat_axis=0, tiled=True)
    field = jnp.take(field, position, axis=0, mode="clip")
    field = lax.all_to_all(field, "dir", split_axis=0, concat_axis=1, tiled=True)
    moved = field[:, :bands].reshape(phonon_heat_density.shape)
    home = mode_heat_magnitude[:, None, None, None] / jnp.expm1(
        mode_pulsation[:, None, None, None] / kelvin[None]
    )
    out = moved + relax_rate[None, :, None, None, None] * (home[None] - moved)
    return out, kelvin


def solution(mesh):
    in_specs = (
        P("dir", None, "space", None, None),
        P(),
        P(),
        P(),
        P(),
        P(),
        P(),
        P(),
        P("space", None),
        P("space"),
        P("space", None, None),
    )
    out_specs = (P("dir", None, "space", None, None), P("space", None, None))
    return jax.shard_map(
        on_device, mesh=mesh, in_specs=in_specs, out_specs=out_specs, check_vma=False
    )
```

time: 1160 us -> 529 us (0.46)
  waiting for transfers between devices: 503 us -> 174 us
  local copies, waits for them, and re-layouts: 252 us -> 44.4 us
  other arithmetic: 139 us -> 21.1 us
  Pallas kernels: 0 us -> 30.5 us
    ppermute x9 -> x0, waiting for transfers between devices: 449 us -> none  [the longest x5 224 us: shifted(): lax.ppermute(shard, axis, [(i, (i + by) % count) for i in range(count)])]
    all_to_all x3 -> x0, blocking collectives: 184 us -> none  [the longest x2 125 us: through_dirs(): lax.all_to_all(result, 'dir', split_axis=0, concat_axis=1, tiled=True)]
    psum x2, blocking collectives: 41.1 us -> 173 us  [on_device(): source = lax.psum(source, ('space', 'dir'))]
    all_to_all x1 -> x4, waiting for transfers between devices: 54.1 us -> 174 us  [the longest x1 115 us: on_device(): lax.all_to_all(field, 'dir', split_axis=1, concat_axis=0, tiled=True)]
    slice x21 -> x1, local copies, waits for them, and re-layouts: 116 us -> 0.07 us  [on_device(): order.reshape(orbits, OCT)[:, OCT - 1]]
    add x9 -> x2, other arithmetic: 104 us -> 6.28 us  [the longest x1 6.28 us: on_device(): out = moved + relax_rate[None, :, None, None, None] * (home[None] - moved)]
    all_gather x0 -> x1, blocking collectives: none -> 58 us  [on_device(): lax.all_gather(own_facets.reshape(rows, deep), 'space').astype(jnp.int32)]
    reshape x12 -> x5, local copies, waits for them, and re-layouts: 64.8 us -> 20 us  [the longest x2 12.8 us: on_device(): field = phonon_heat_density.reshape(local_dirs, bands, rows, deep)]
  transfers between devices with their start and end apart: 10 -> 4, of which waited for: 10 -> 2; matrix products, arithmetic and copies ran while one was open for 0% -> 2% of each run, Pallas kernels for 0% -> 0%
where the time goes in v1:
time: 529 us; the launch traced here: 527 us
  blocking collectives  231 us (44%)
  waiting for transfers between devices  174 us (33%)
  local copies, waits for them, and re-layouts  44.4 us (8%)
  Pallas kernels  30.5 us (6%)
  starting transfers between devices  23.8 us (4%)
  other arithmetic  21.1 us (4%)
    psum x2, blocking collectives, on_device(): source = lax.psum(source, ('space', 'dir'))  173 us
    all_to_all x1, waiting for transfers between devices, on_device(): lax.all_to_all(field, 'dir', split_axis=1, concat_axis=0, tiled=True)  115 us
    all_to_all x2, waiting for transfers between devices, on_device(): lax.all_to_all(field, 'space', split_axis=0, concat_axis=0, tiled=True)  59.4 us
    all_gather x1, blocking collectives, on_device(): lax.all_gather(own_facets.reshape(rows, deep), 'space').astype(jnp.int32)  58 us
    pallas_call x2, Pallas kernels, sweep(): pl.pallas_call(functools.partial(sweep_kernel, high, tiles, bose is not N...  30.5 us
    reshape x2, local copies, waits for them, and re-layouts, on_device(): field = phonon_heat_density.reshape(local_dirs, bands, rows, deep)  12.8 us
  transfers between devices with their start and end apart: 4, of which 2 were waited for; matrix products, arithmetic and copies ran while one was open for 2% of the time, Pallas kernels for 0%

profile of v1, /device:TPU:0, one launch (start us, length us, event | category | flops | bytes accessed | tf_op | source)
XLA Modules:
  0.0 527.3 jit_solution(14200764864762959878)
XLA Ops:
  0.6 7.3 %reshape.795 = f32[16,40,8,256]{3,2,1,0:T(8,128)} reshape(f32[16,40,2,4,256]{4,3,2,1,0:T(4,128)} %param.11) | data formatting | bytes 10485760 | tf_op jit(solution)/shard_map/reshape | solution.py:215
  7.9 5.6 %copy.85 = f32[16,40,8,256]{3,2,0,1:T(8,128)} copy(f32[16,40,8,256]{3,2,1,0:T(8,128)} %reshape.795) | data formatting | bytes 10485760 | tf_op jit(solution)/shard_map/reshape | solution.py:215
  13.4 7.4 %all-to-all-start = ((f32[16,40,8,256]{3,2,0,1:T(8,128)}), f32[16,40,8,256]{3,2,0,1:T(8,128)}, u32[]{:S(2)}, u32[]{:S(2)}) async-start(f32[16,40,8,256]{3,2,0,1:T(8,128)} %copy.85), calls=%async_computation | async-start | bytes 10485760 | tf_op jit(solution)/shard_map/all_to_all | solution.py:217
  20.9 0.1 select_reduce_fusion.5
  21.0 0.2 select_reduce_fusion.4
  21.2 0.2 select_reduce_fusion.3
  21.4 0.2 select_reduce_fusion.2
  21.6 0.1 select_reduce_fusion.1
  21.8 114.9 %all-to-all-done = f32[16,40,8,256]{3,2,0,1:T(8,128)} async-done(((f32[16,40,8,256]{3,2,0,1:T(8,128)}), f32[16,40,8,256]{3,2,0,1:T(8,128)}, u32[]{:S(2)}, u32[]{:S(2)}) %all-to-all-start) | async-done | bytes 5242912 | tf_op jit(solution)/shard_map/all_to_all | solution.py:217
  136.6 5.3 %copy.83 = f32[8,16,5,8,256]{4,3,2,1,0:T(8,128)} copy(f32[8,16,5,8,256]{4,3,1,2,0:T(8,128)} %bitcast.17) | data formatting | bytes 10485760 | tf_op jit(solution)/shard_map/all_to_all | solution.py:217
  142.0 5.7 %gather_fusion = f32[128,5,8,256]{3,2,1,0:T(8,128)} fusion(f32[128,5,8,256]{3,2,1,0:T(8,128)} %bitcast.63, s32[1024]{0:T(1024)S(1)} %pad_clamp_fusion.1), kind=kCustom, calls=%fused_computation | custom fusion | bytes 10486272 | tf_op jit(solution)/shard_map/jit(_take)/gather | solution.py:218
  147.7 5.2 all-to-all-start.1
  153.3 0.1 dynamic-slice_reduce_fusion
  153.5 0.2 select_reduce_fusion.6
  154.1 0.1 mul.674
  154.2 0.1 mul.676
  154.2 0.1 copy.80
  154.3 0.1 copy.79
  155.2 0.1 select_reduce_fusion
  155.3 58.0 %all_gather.3 = f32[4,8,256]{2,1,0:T(8,128)S(1)} all-gather(f32[1,8,256]{2,1,0:T(8,128)S(1)} %convert_element_type.21), channel_id=1, replica_groups=mesh['space'=4,'dir'=8] {'space'}, dimensions={0}, use_global_device_ids=true | all-gather | bytes 40960 | tf_op jit(solution)/shard_map/all_gather | solution.py:194
  213.3 0.6 convert_element_type.22.facet_ref
  214.1 0.7 stack.2.coef_ref
  214.8 0.6 divide_reduce_fusion.6
  215.4 15.0 %shard_map.122 = (f32[4,32,5,8,256]{4,3,2,1,0:T(8,128)}, f32[4,8,256]{2,1,0:T(8,128)}) custom-call(f32[20,11]{1,0:T(8,128)} %stack.2.coef_ref, s32[4,8,256]{2,1,0:T(8,128)} %convert_element_type.22.facet_ref, f32[4,32,5,8,256]{4,3,2,1,0:T(8,128)} %bitcast.19.e_ref), custom_call_target="tpu_custom_call" | custom-call | tf_op jit(solution)/shard_map/pallas_call | solution.py:118
  230.5 37.8 %psum.14 = f32[4,8,256]{2,1,0:T(8,128)S(1)} all-reduce(f32[4,8,256]{2,1,0:T(8,128)} %get-tuple-element.7), channel_id=1, replica_groups=mesh['space'=4,'dir'=8] {'space','dir'}, use_global_device_ids=true, to_apply=%region_11.12 | all-reduce | flops 8192 | bytes 65536 | tf_op jit(solution)/shard_map/psum | solution.py:226
  268.3 1.2 subtract_clamp_fusion
  269.5 1.0 divide_reduce_fusion.2
  270.5 1.2 maximum_minimum_fusion.2
  271.8 1.0 divide_reduce_fusion.1
  272.9 1.0 divide_reduce_fusion
  273.9 1.3 maximum_minimum_fusion
  275.2 0.8 fusion.7.rest_0_
  276.0 15.5 %shard_map.123 = (f32[4,32,5,8,256]{4,3,2,1,0:T(8,128)}, f32[4,8,256]{2,1,0:T(8,128)}) custom-call(f32[20,11]{1,0:T(8,128)} %stack.2.coef_ref, s32[4,8,256]{2,1,0:T(8,128)} %convert_element_type.22.facet_ref, f32[4,32,5,8,256]{4,3,2,1,0:T(8,128)} %get-tuple-element.6.e_ref, f32[5,4,8,256]{3,2,1,0:T(8,128)} %fusion.7.rest_0_), custom_call_target="tpu_custom_call" | custom-call | tf_op jit(solution)/shard_map/pallas_call | solution.py:118
  291.4 5.1 all-to-all-start.2
  296.5 59.4 %all-to-all-done.2 = f32[128,5,8,256]{3,2,1,0:T(8,128)} async-done(((f32[128,5,8,256]{3,2,1,0:T(8,128)}), f32[128,5,8,256]{3,2,1,0:T(8,128)}, u32[]{:S(2)}, u32[]{:S(2)}) %all-to-all-start.2) | async-done | bytes 5242912 | tf_op jit(solution)/shard_map/all_to_all | solution.py:238
  355.9 5.7 %gather_fusion.1 = f32[128,5,8,256]{3,2,1,0:T(8,128)} fusion(f32[128,5,8,256]{3,2,1,0:T(8,128)} %all-to-all-done.2, s32[1024]{0:T(1024)S(1)} %pad_clamp_fusion), kind=kCustom, calls=%fused_computation.1 | custom fusion | bytes 10486272 | tf_op jit(solution)/shard_map/jit(_take)/gather | solution.py:239
  361.7 6.1 %all-to-all-start.3 = ((f32[128,5,8,256]{3,2,1,0:T(8,128)}), f32[128,5,8,256]{3,2,1,0:T(8,128)}, u32[]{:S(2)}, u32[]{:S(2)}) async-start(f32[128,5,8,256]{3,2,1,0:T(8,128)} %gather_fusion.1), calls=%async_computation.3 | async-start | bytes 10485760 | tf_op jit(solution)/shard_map/all_to_all | solution.py:240
  367.8 135.5 %psum.15 = f32[4,8,256]{2,1,0:T(8,128)S(1)} all-reduce(f32[4,8,256]{2,1,0:T(8,128)S(1)} %copy-done), channel_id=1, replica_groups=mesh['space'=4,'dir'=8] {'space','dir'}, use_global_device_ids=true, to_apply=%region_19.20 | all-reduce | flops 8192 | bytes 65536 | tf_op jit(solution)/shard_map/psum | solution.py:226
  503.4 1.2 subtract_clamp_fusion.1
  504.6 0.3 divide_reduce_fusion.5
  504.9 1.2 maximum_minimum_fusion.5
  506.2 0.3 divide_reduce_fusion.4
  506.5 0.3 divide_reduce_fusion.3
  506.9 1.2 maximum_minimum_fusion.3
  508.1 0.3 fusion.3
  508.5 5.4 %copy.90 = f32[8,16,5,8,256]{4,3,2,0,1:T(8,128)} copy(f32[8,16,5,8,256]{4,3,2,1,0:T(8,128)} %bitcast.24) | data formatting | bytes 10485760 | tf_op jit(solution)/shard_map/all_to_all | solution.py:240
  513.9 7.1 %reshape.775 = f32[16,40,2,4,256]{4,3,2,1,0:T(4,128)} reshape(f32[16,8,5,8,256]{4,3,2,1,0:T(8,128)} %bitcast.64) | data formatting | bytes 10485760 | tf_op jit(solution)/shard_map/reshape | solution.py:241
  521.0 6.3 %multiply_add_fusion = f32[16,40,2,4,256]{4,3,2,1,0:T(4,128)} fusion(f32[16,40,2,4,256]{4,3,2,1,0:T(4,128)} %reshape.775, f32[40,2,4,256]{3,2,1,0:T(4,128)S(1)} %fusion.3, f32[40]{0:T(128)S(1)} %copy-done.6), kind=kLoop, calls=%fused_computation.3 | loop fusion | flops 3932160 | bytes 10813600 | tf_op jit(solution)/shard_map/add | solution.py:245
  (79 shorter events, 1.3 us)
Async XLA Ops:
  13.4 7.4 %copy-start.7 = (s32[3,128]{1,0:T(4,128)S(1)}, s32[3,128]{1,0:T(4,128)}, u32[]{:S(2)}) copy-start(s32[3,128]{1,0:T(4,128)} %param.14) | copy-start | bytes 4612
  13.4 7.6 %copy-start.3 = (f32[3,128]{1,0:T(4,128)S(1)}, f32[3,128]{1,0:T(4,128)}, u32[]{:S(2)}) copy-start(f32[3,128]{1,0:T(4,128)} %param.12) | copy-start | bytes 4612
  13.4 123.2 %all-to-all-start = ((f32[16,40,8,256]{3,2,0,1:T(8,128)}), f32[16,40,8,256]{3,2,0,1:T(8,128)}, u32[]{:S(2)}, u32[]{:S(2)}) async-start(f32[16,40,8,256]{3,2,0,1:T(8,128)} %copy.85), calls=%async_computation | async-start | bytes 10485760 | tf_op jit(solution)/shard_map/all_to_all | solution.py:217
  147.7 5.3 %copy-start.10 = (f32[40]{0:T(128)S(1)}, f32[40]{0:T(128)}, u32[]{:S(2)}) copy-start(f32[40]{0:T(128)} %param.15) | copy-start | bytes 484
  147.7 5.8 %copy-start.8 = (f32[128]{0:T(128)S(1)}, f32[128]{0:T(128)}, u32[]{:S(2)}) copy-start(f32[128]{0:T(128)} %param.13) | copy-start | bytes 1540
  147.7 6.2 %copy-start.6 = (f32[40]{0:T(128)S(1)}, f32[40]{0:T(128)}, u32[]{:S(2)}) copy-start(f32[40]{0:T(128)} %param.16) | copy-start | bytes 484
  147.7 7.4 %copy-start.9 = (s32[1,16]{1,0:T(1,128)S(1)}, s32[1,16]{1,0:T(1,128)}, u32[]{:S(2)}) copy-start(s32[1,16]{1,0:T(1,128)} %param.19) | copy-start | bytes 196
  147.7 7.4 %copy-start.2 = (s32[1,16,128]{2,1,0:T(8,128)S(1)}, s32[1,16,128]{2,1,0:T(8,128)}, u32[]{:S(2)}) copy-start(s32[1,16,128]{2,1,0:T(8,128)} %param.21) | copy-start | bytes 24580
  147.7 66.2 %copy-start.4 = (f32[40]{0:T(128)S(1)}, f32[40]{0:T(128)}, u32[]{:S(2)}) copy-start(f32[40]{0:T(128)} %param.18) | copy-start | bytes 484
  147.7 66.3 %copy-start.5 = (f32[40]{0:T(128)S(1)}, f32[40]{0:T(128)}, u32[]{:S(2)}) copy-start(f32[40]{0:T(128)} %param.17) | copy-start | bytes 484
  147.7 67.7 %all-to-all-start.1 = ((f32[128,5,8,256]{3,2,1,0:T(8,128)}), f32[128,5,8,256]{3,2,1,0:T(8,128)}, u32[]{:S(2)}, u32[]{:S(2)}) async-start(f32[128,5,8,256]{3,2,1,0:T(8,128)} %gather_fusion), calls=%async_computation.1 | async-start | bytes 10485760 | tf_op jit(solution)/shard_map/all_to_all | solution.py:219
  291.4 64.5 %all-to-all-start.2 = ((f32[128,5,8,256]{3,2,1,0:T(8,128)}), f32[128,5,8,256]{3,2,1,0:T(8,128)}, u32[]{:S(2)}, u32[]{:S(2)}) async-start(f32[128,5,8,256]{3,2,1,0:T(8,128)} %bitcast.65), calls=%async_computation.2 | async-start | bytes 10485760 | tf_op jit(solution)/shard_map/all_to_all | solution.py:238
  361.7 6.1 %copy-start = (f32[4,8,256]{2,1,0:T(8,128)S(1)}, f32[4,8,256]{2,1,0:T(8,128)}, u32[]{:S(2)}) copy-start(f32[4,8,256]{2,1,0:T(8,128)} %get-tuple-element.9) | copy-start | bytes 98308
  361.7 146.8 %all-to-all-start.3 = ((f32[128,5,8,256]{3,2,1,0:T(8,128)}), f32[128,5,8,256]{3,2,1,0:T(8,128)}, u32[]{:S(2)}, u32[]{:S(2)}) async-start(f32[128,5,8,256]{3,2,1,0:T(8,128)} %gather_fusion.1), calls=%async_computation.3 | async-start | bytes 10485760 | tf_op jit(solution)/shard_map/all_to_all | solution.py:240
  508.1 5.8 %copy-start.1 = (f32[2,4,256]{2,1,0:T(4,128)}, f32[2,4,256]{2,1,0:T(4,128)S(1)}, u32[]{:S(2)}) copy-start(f32[2,4,256]{2,1,0:T(4,128)S(1)} %maximum_minimum_fusion.3) | copy-start | bytes 24580

commit v2 on v1

--- a/solution.py
+++ b/solution.py
@@ -129,6 +129,326 @@
     )(*operands)
 
 
+MESH = pl.DeviceIdType.MESH
+
+
+def greet(tile, tiles, group, groups):
+    barrier = pltpu.get_barrier_semaphore()
+    for u in range(1, tiles):
+        pl.semaphore_signal(
+            barrier, inc=1, device_id=(lax.rem(tile + u, tiles), group), device_id_type=MESH
+        )
+    for t in range(1, groups):
+        pl.semaphore_signal(
+            barrier, inc=1, device_id=(tile, lax.rem(group + t, groups)), device_id_type=MESH
+        )
+    pl.semaphore_wait(barrier, tiles + groups - 2)
+
+
+def remote(src, dst, send, recv, device):
+    return pltpu.make_async_remote_copy(
+        src_ref=src, dst_ref=dst, send_sem=send, recv_sem=recv, device_id=device, device_id_type=MESH
+    )
+
+
+def spread_kernel(
+    tiles, groups, order_ref, facet_ref, home_ref, field_ref, facets_ref, *scratch
+):
+    share = field_ref.shape[2]
+    landed, sorted_refs = scratch[:share], scratch[share : 2 * share]
+    dir_send, dir_recv, tile_send, tile_recv, facet_send, facet_recv, own_sem = scratch[2 * share :]
+    local_dirs, _, wide, high, _ = home_ref.shape
+    dirs, part = landed[0].shape[0], field_ref.shape[1]
+    tile, group = lax.axis_index("space"), lax.axis_index("dir")
+
+    own = [
+        pltpu.make_async_copy(
+            home_ref.at[:, group * share + k],
+            landed[k].at[pl.ds(group * local_dirs, local_dirs)],
+            own_sem.at[k],
+        )
+        for k in range(share)
+    ]
+    for copy in own:
+        copy.start()
+    own_facets = pltpu.make_async_copy(facet_ref, facets_ref.at[tile], own_sem.at[2 * share])
+    own_facets.start()
+    greet(tile, tiles, group, groups)
+
+    first = []
+    for k in range(share):
+        line = []
+        for t in range(1, groups):
+            peer = lax.rem(group + t, groups)
+            copy = remote(
+                home_ref.at[:, peer * share + k],
+                landed[k].at[pl.ds(group * local_dirs, local_dirs)],
+                dir_send.at[k, t],
+                dir_recv.at[k, t],
+                (tile, peer),
+            )
+            copy.start()
+            line.append(copy)
+        first.append(line)
+    third = []
+    for u in range(1, tiles):
+        copy = remote(
+            facet_ref,
+            facets_ref.at[tile],
+            facet_send.at[u],
+            facet_recv.at[u],
+            (lax.rem(tile + u, tiles), group),
+        )
+        copy.start()
+        third.append(copy)
+
+    second, kept = [], []
+    for k in range(share):
+        own[k].wait()
+        for copy in first[k]:
+            copy.wait_recv()
+
+        def move(j, carry):
+            d = order_ref[j]
+            for x in range(wide):
+                sorted_refs[k][j, x * high : (x + 1) * high, :] = landed[k][d, x]
+            return carry
+
+        lax.fori_loop(0, dirs, move, 0, unroll=4)
+        for u in range(1, tiles):
+            peer = lax.rem(tile + u, tiles)
+            copy = remote(
+                sorted_refs[k].at[pl.ds(peer * part, part)],
+                field_ref.at[tile, :, k],
+                tile_send.at[k, u],
+                tile_recv.at[k, u],
+                (peer, group),
+            )
+            copy.start()
+            second.append(copy)
+        copy = pltpu.make_async_copy(
+            sorted_refs[k].at[pl.ds(tile * part, part)],
+            field_ref.at[tile, :, k],
+            own_sem.at[share + k],
+        )
+        copy.start()
+        kept.append(copy)
+    own_facets.wait()
+    for copy in kept:
+        copy.wait()
+    for copy in second + third:
+        copy.wait_recv()
+    for line in first:
+        for copy in line:
+            copy.wait_send()
+    for copy in second + third:
+        copy.wait_send()
+
+
+def spread(tiles, groups, share, order, facets, home):
+    local_dirs, _, wide, high, deep = home.shape
+    dirs, rows = local_dirs * groups, wide * high
+    part = dirs // tiles
+    vmem = pl.BlockSpec(memory_space=pltpu.VMEM)
+    anywhere = pl.BlockSpec(memory_space=pl.ANY)
+    dma = pltpu.SemaphoreType.DMA
+    return pl.pallas_call(
+        functools.partial(spread_kernel, tiles, groups),
+        in_specs=[pl.BlockSpec(memory_space=pltpu.SMEM), vmem, anywhere],
+        out_specs=[anywhere, vmem],
+        out_shape=[
+            jax.ShapeDtypeStruct((tiles, part, share, rows, deep), jnp.float32),
+            jax.ShapeDtypeStruct((tiles, rows, deep), jnp.float32),
+        ],
+        scratch_shapes=[pltpu.VMEM((dirs, wide, high, deep), jnp.float32)] * share
+        + [pltpu.VMEM((dirs, rows, deep), jnp.float32)] * share
+        + [
+            dma((share, groups)),
+            dma((share, groups)),
+            dma((share, tiles)),
+            dma((share, tiles)),
+            dma((tiles,)),
+            dma((tiles,)),
+            dma((2 * share + 1,)),
+        ],
+        compiler_params=pltpu.CompilerParams(collective_id=0, has_side_effects=True),
+    )(order, facets, home)
+
+
+def collect_kernel(tiles, groups, position_ref, field_ref, home_ref, *scratch):
+    share = field_ref.shape[2]
+    landed, sorted_refs = scratch[:share], scratch[share : 2 * share]
+    dir_send, dir_recv, tile_send, tile_recv, own_sem = scratch[2 * share :]
+    local_dirs, _, wide, high, _ = home_ref.shape
+    dirs, part = landed[0].shape[0], field_ref.shape[1]
+    tile, group = lax.axis_index("space"), lax.axis_index("dir")
+    own = [
+        pltpu.make_async_copy(
+            field_ref.at[tile, :, k], landed[k].at[pl.ds(tile * part, part)], own_sem.at[k]
+        )
+        for k in range(share)
+    ]
+    for copy in own:
+        copy.start()
+    greet(tile, tiles, group, groups)
+    first = []
+    for k in range(share):
+        line = []
+        for u in range(1, tiles):
+            peer = lax.rem(tile + u, tiles)
+            copy = remote(
+                field_ref.at[peer, :, k],
+                landed[k].at[pl.ds(tile * part, part)],
+                tile_send.at[k, u],
+                tile_recv.at[k, u],
+                (peer, group),
+            )
+            copy.start()
+            line.append(copy)
+        first.append(line)
+    second, kept = [], []
+    for k in range(share):
+        own[k].wait()
+        for copy in first[k]:
+            copy.wait_recv()
+
+        def move(d, carry):
+            j = position_ref[d]
+            for x in range(wide):
+                sorted_refs[k][d, x] = landed[k][j, x * high : (x + 1) * high, :]
+            return carry
+
+        lax.fori_loop(0, dirs, move, 0, unroll=4)
+        for t in range(1, groups):
+            peer = lax.rem(group + t, groups)
+            copy = remote(
+                sorted_refs[k].at[pl.ds(peer * local_dirs, local_dirs)],
+                home_ref.at[:, group * share + k],
+                dir_send.at[k, t],
+                dir_recv.at[k, t],
+                (tile, peer),
+            )
+            copy.start()
+            second.append(copy)
+        copy = pltpu.make_async_copy(
+            sorted_refs[k].at[pl.ds(group * local_dirs, local_dirs)],
+            home_ref.at[:, group * share + k],
+            own_sem.at[share + k],
+        )
+        copy.start()
+        kept.append(copy)
+    for copy in kept:
+        copy.wait()
+    for copy in second:
+        copy.wait_recv()
+    for line in first:
+        for copy in line:
+            copy.wait_send()
+    for copy in second:
+        copy.wait_send()
+
+
+def collect(tiles, groups, position, field, high):
+    _, part, share, rows, deep = field.shape
+    dirs = part * tiles
+    local_dirs, wide = dirs // groups, rows // high
+    anywhere = pl.BlockSpec(memory_space=pl.ANY)
+    dma = pltpu.SemaphoreType.DMA
+    return pl.pallas_call(
+        functools.partial(collect_kernel, tiles, groups),
+        in_specs=[pl.BlockSpec(memory_space=pltpu.SMEM), anywhere],
+        out_specs=anywhere,
+        out_shape=jax.ShapeDtypeStruct(
+            (local_dirs, share * groups, wide, high, deep), jnp.float32
+        ),
+        scratch_shapes=[pltpu.VMEM((dirs, rows, deep), jnp.float32)] * share
+        + [pltpu.VMEM((dirs, wide, high, deep), jnp.float32)] * share
+        + [
+            dma((share, groups)),
+            dma((share, groups)),
+            dma((share, tiles)),
+            dma((share, tiles)),
+            dma((2 * share,)),
+        ],
+        compiler_params=pltpu.CompilerParams(collective_id=1, has_side_effects=True),
+    )(position, field)
+
+
+def total_kernel(tiles, groups, everywhere, part_ref, total_ref, near, own, far, summed, *sems):
+    near_send, near_recv, far_send, far_recv, last_send, last_recv = sems
+    tile, group = lax.axis_index("space"), lax.axis_index("dir")
+    greet(tile, tiles, group, groups)
+    copies = []
+    for u in range(1, tiles):
+        peer = lax.rem(tile + u, tiles)
+        copy = remote(
+            part_ref.at[peer], near.at[u], near_send.at[u], near_recv.at[u], (peer, group)
+        )
+        copy.start()
+        copies.append(copy)
+    value = part_ref[tile]
+    for u in range(1, tiles):
+        copies[u - 1].wait_recv()
+        value = value + near[u]
+    own[...] = value
+    gathers = []
+    for t in range(1, groups):
+        peer = lax.rem(group + t, groups)
+        copy = remote(own, far.at[group], far_send.at[t], far_recv.at[t], (tile, peer))
+        copy.start()
+        gathers.append(copy)
+    far[group] = value
+    for copy in gathers:
+        copy.wait_recv()
+    value = far[0]
+    for g in range(1, groups):
+        value = value + far[g]
+    lasts = []
+    if everywhere:
+        summed[...] = value
+        for u in range(1, tiles):
+            peer = lax.rem(tile + u, tiles)
+            copy = remote(
+                summed, total_ref.at[tile], last_send.at[u], last_recv.at[u], (peer, group)
+            )
+            copy.start()
+            lasts.append(copy)
+        total_ref[tile] = value
+        for copy in lasts:
+            copy.wait_recv()
+    else:
+        total_ref[0] = value
+    for copy in copies + gathers + lasts:
+        copy.wait_send()
+
+
+def total(tiles, groups, everywhere, source):
+    _, rows, deep = source.shape
+    vmem = pl.BlockSpec(memory_space=pltpu.VMEM)
+    dma = pltpu.SemaphoreType.DMA
+    return pl.pallas_call(
+        functools.partial(total_kernel, tiles, groups, everywhere),
+        in_specs=[vmem],
+        out_specs=vmem,
+        out_shape=jax.ShapeDtypeStruct((tiles if everywhere else 1, rows, deep), jnp.float32),
+        scratch_shapes=[
+            pltpu.VMEM((tiles, rows, deep), jnp.float32),
+            pltpu.VMEM((rows, deep), jnp.float32),
+            pltpu.VMEM((groups, rows, deep), jnp.float32),
+            pltpu.VMEM((rows, deep), jnp.float32),
+            dma((tiles,)),
+            dma((tiles,)),
+            dma((groups,)),
+            dma((groups,)),
+            dma((tiles,)),
+            dma((tiles,)),
+        ],
+        compiler_params=pltpu.CompilerParams(
+            collective_id=2 if everywhere else 3, has_side_effects=True
+        ),
+    )(source)
+
+
 def beam_coeffs(abs_speed):
     return (
         1.0 - 1.5 * abs_speed + 0.5 * abs_speed * abs_speed,
@@ -191,8 +511,6 @@
     own_facets = facet_grid(
         wall_blocks[0], wall_count[0], wall_facet[0], wide * high * deep // BLOCK
     ).astype(jnp.float32)
-    facets = lax.all_gather(own_facets.reshape(rows, deep), "space").astype(jnp.int32)
-
     def own_bands(values):
         return lax.dynamic_slice_in_dim(jnp.pad(values, (0, extra)), group * share, share)
 
@@ -212,18 +530,17 @@
     columns.append(jnp.broadcast_to(rates[:, None], columns[0].shape))
     coefs = jnp.stack(columns, axis=-1).reshape(share * part_orbits, len(columns))
 
-    field = phonon_heat_density.reshape(local_dirs, bands, rows, deep)
-    field = jnp.pad(field, ((0, 0), (0, extra), (0, 0), (0, 0)))
-    field = lax.all_to_all(field, "dir", split_axis=1, concat_axis=0, tiled=True)
-    field = jnp.take(field, order, axis=0, mode="clip")
-    field = lax.all_to_all(field, "space", split_axis=0, concat_axis=0, tiled=True)
-    field = field.reshape(tiles, part, share, rows, deep)
+    home = phonon_heat_density
+    if extra:
+        home = jnp.pad(home, ((0, 0), (0, extra), (0, 0), (0, 0), (0, 0)))
+    field, facets = spread(tiles, groups, share, order, own_facets.reshape(rows, deep), home)
+    facets = facets.astype(jnp.int32)
 
     collision_speed_factor = relax_rate * mode_heat_magnitude
     bose = None
     for step_num in range(STEPS):
         field, source = sweep(high, coefs, facets, field, bose)
-        source = lax.psum(source, ("space", "dir"))
+        source = total(tiles, groups, step_num < STEPS - 1, source)
         if step_num < STEPS - 1:
             kelvin = root_finder_guess(
                 source.reshape(-1), collision_speed_factor, mode_pulsation
@@ -231,14 +548,9 @@
             bose = magnitudes[:, None, None, None] / jnp.expm1(
                 pulsations[:, None, None, None] / kelvin[None]
             )
-    own_source = lax.dynamic_index_in_dim(source, tile, 0, keepdims=False)
-    kelvin = root_finder_guess(own_source.reshape(-1), collision_speed_factor, mode_pulsation)
+    kelvin = root_finder_guess(source.reshape(-1), collision_speed_factor, mode_pulsation)
     kelvin = kelvin.reshape(wide, high, deep)
-    field = field.reshape(dirs, share, rows, deep)
-    field = lax.all_to_all(field, "space", split_axis=0, concat_axis=0, tiled=True)
-    field = jnp.take(field, position, axis=0, mode="clip")
-    field = lax.all_to_all(field, "dir", split_axis=0, concat_axis=1, tiled=True)
-    moved = field[:, :bands].reshape(phonon_heat_density.shape)
+    moved = collect(tiles, groups, position, field, high)[:, :bands]
     home = mode_heat_magnitude[:, None, None, None] / jnp.expm1(
         mode_pulsation[:, None, None, None] / kelvin[None]
     )

time: 529 us -> 355 us (0.67)
  Pallas kernels: 30.5 us -> 316 us
  blocking collectives: 231 us -> 0 us
  waiting for transfers between devices: 174 us -> 0 us
  local copies, waits for them, and re-layouts: 44.4 us -> 9.21 us
  starting transfers between devices: 23.8 us -> 0 us
    pallas_call x0 -> x4, Pallas kernels: none -> 286 us  [the longest x1 126 us: spread(): pl.pallas_call(functools.partial(spread_kernel, tiles, groups), in_specs=...]
    all_to_all x4 -> x0, waiting for transfers between devices: 174 us -> none  [the longest x1 115 us: on_device(): lax.all_to_all(field, 'dir', split_axis=1, concat_axis=0, tiled=True)]
    psum x2 -> x0, blocking collectives: 173 us -> none  [on_device(): source = lax.psum(source, ('space', 'dir'))]
    all_gather x1 -> x0, blocking collectives: 58 us -> none  [on_device(): lax.all_gather(own_facets.reshape(rows, deep), 'space').astype(jnp.int32)]
    all_to_all x4 -> x0, starting transfers between devices: 23.8 us -> none  [the longest x2 10.3 us: on_device(): lax.all_to_all(field, 'space', split_axis=0, concat_axis=0, tiled=True)]
    reshape x4 -> x1, local copies, waits for them, and re-layouts: 19.9 us -> 0.71 us  [on_device(): source.reshape(-1)]
    gather x2 -> x0, local copies, waits for them, and re-layouts: 11.4 us -> none  [the longest x1 5.73 us: on_device(): field = jnp.take(field, position, axis=0, mode='clip')]
    all_to_all x2 -> x0, local copies, waits for them, and re-layouts: 10.8 us -> none  [the longest x1 5.44 us: on_device(): lax.all_to_all(field, 'dir', split_axis=0, concat_axis=1, tiled=True)]
  transfers between devices with their start and end apart: 4 -> 0, of which waited for: 2 -> 0; matrix products, arithmetic and copies ran while one was open for 2% -> 0% of each run, Pallas kernels for 0% -> 0%
where the time goes in v2:
time: 355 us; the launch traced here: 353 us
  Pallas kernels  316 us (89%)
  other arithmetic  26.1 us (7%)
  local copies, waits for them, and re-layouts  9.21 us (3%)
    pallas_call x1, Pallas kernels, spread(): pl.pallas_call(functools.partial(spread_kernel, tiles, groups), in_specs=...  126 us
    pallas_call x1, Pallas kernels, collect(): pl.pallas_call(functools.partial(collect_kernel, tiles, groups), in_specs...  119 us
    pallas_call x2, Pallas kernels, total(): pl.pallas_call(functools.partial(total_kernel, tiles, groups, everywhere)...  40.7 us
    pallas_call x2, Pallas kernels, sweep(): pl.pallas_call(functools.partial(sweep_kernel, high, tiles, bose is not N...  30.5 us
    min x8, other arithmetic, root_finder_guess(): jnp.clip(pseudo_kelvin_field - mismatch_error / gradient_guess, 0.5 * pse...  7.64 us

profile of v2, /device:TPU:0, one launch (start us, length us, event | category | flops | bytes accessed | tf_op | source)
XLA Modules:
  0.0 353.4 jit_solution(3191277778874407332)
XLA Ops:
  1.3 0.7 dynamic_slice.15
  2.0 0.7 dynamic_slice.17
  2.8 0.7 dynamic_slice.18
  3.5 0.7 dynamic_slice.19
  4.2 0.7 fusion.12
  4.9 0.8 slice_bitcast_fusion.3
  5.7 0.1 select_reduce_fusion.5
  5.8 0.8 slice_bitcast_fusion.2
  6.6 1.4 divide_reduce_fusion.6
  8.0 0.7 compare_convert_fusion
  8.7 0.2 select_reduce_fusion.4
  8.9 0.2 select_reduce_fusion.3
  9.1 0.2 select_reduce_fusion.2
  9.3 0.5 bitcast_add_fusion.1.position_ref
  9.8 0.1 select_reduce_fusion.1.order_ref
  10.0 0.1 mul.650
  10.1 0.8 select_reduce_fusion
  11.0 0.6 convert_element_type.15.facet_ref
  11.8 0.1 dynamic-slice_reduce_fusion
  11.9 0.9 select_reduce_fusion.6
  13.2 0.1 copy.50
  13.3 0.1 copy.49
  13.4 0.7 stack.2.coef_ref
  14.1 125.8 %shard_map.122 = (f32[4,32,5,8,256]{4,3,2,1,0:T(8,128)}, f32[4,8,256]{2,1,0:T(8,128)}) custom-call(s32[128]{0:T(128)} %copy-done.5, f32[8,256]{1,0:T(8,128)} %convert_element_type.15.facet_ref, f32[16,40,2,4,256]{4,3,2,1,0:T(4,128)} %home_ref.1), custom_call_target="tpu_custom_call" | custom-call | tf_op jit(solution)/shard_map/pallas_call | solution.py:255
  139.9 1.4 convert_element_type.16.facet_ref
  141.2 15.0 %shard_map.123 = (f32[4,32,5,8,256]{4,3,2,1,0:T(8,128)}, f32[4,8,256]{2,1,0:T(8,128)}) custom-call(f32[20,11]{1,0:T(8,128)} %stack.2.coef_ref, s32[4,8,256]{2,1,0:T(8,128)} %convert_element_type.16.facet_ref, f32[4,32,5,8,256]{4,3,2,1,0:T(8,128)} %get-tuple-element.9.e_ref), custom_call_target="tpu_custom_call" | custom-call | tf_op jit(solution)/shard_map/pallas_call | solution.py:118
  156.3 22.0 %shard_map.124 = f32[4,8,256]{2,1,0:T(8,128)} custom-call(f32[4,8,256]{2,1,0:T(8,128)} %get-tuple-element.11.part_ref), custom_call_target="tpu_custom_call" | custom-call | tf_op jit(solution)/shard_map/pallas_call | solution.py:429
  178.3 0.8 copy.51
  179.1 1.3 subtract_clamp_fusion
  180.3 1.0 divide_reduce_fusion.2
  181.3 1.3 maximum_minimum_fusion.2
  182.7 1.0 divide_reduce_fusion.1
  183.7 1.0 divide_reduce_fusion
  184.8 1.3 maximum_minimum_fusion
  186.1 0.8 fusion.7.rest_0_
  186.9 15.5 %shard_map.125 = (f32[4,32,5,8,256]{4,3,2,1,0:T(8,128)}, f32[4,8,256]{2,1,0:T(8,128)}) custom-call(f32[20,11]{1,0:T(8,128)} %stack.2.coef_ref, s32[4,8,256]{2,1,0:T(8,128)} %convert_element_type.16.facet_ref, f32[4,32,5,8,256]{4,3,2,1,0:T(8,128)} %get-tuple-element.10.e_ref, f32[5,4,8,256]{3,2,1,0:T(8,128)} %fusion.7.rest_0_), custom_call_target="tpu_custom_call" | custom-call | tf_op jit(solution)/shard_map/pallas_call | solution.py:118
  202.4 119.4 %shard_map.126 = f32[16,40,2,4,256]{4,3,2,1,0:T(4,128)} custom-call(s32[128]{0:T(128)} %bitcast_add_fusion.1.position_ref, f32[4,32,5,8,256]{4,3,2,1,0:T(8,128)} %get-tuple-element.12.field_ref), custom_call_target="tpu_custom_call" | custom-call | tf_op jit(solution)/shard_map/pallas_call | solution.py:357
  321.8 18.7 %shard_map.127 = f32[1,8,256]{2,1,0:T(8,128)} custom-call(f32[4,8,256]{2,1,0:T(8,128)} %get-tuple-element.13.part_ref), custom_call_target="tpu_custom_call" | custom-call | tf_op jit(solution)/shard_map/pallas_call | solution.py:429
  340.5 0.7 copy.52
  341.2 1.3 subtract_clamp_fusion.1
  342.4 0.7 reshape.705
  343.2 0.3 divide_reduce_fusion.5
  343.5 1.3 maximum_minimum_fusion.5
  344.7 0.3 divide_reduce_fusion.4
  345.1 0.3 divide_reduce_fusion.3
  345.4 1.3 maximum_minimum_fusion.3
  346.7 0.3 fusion.3
  347.1 6.3 %multiply_add_fusion = f32[16,40,2,4,256]{4,3,2,1,0:T(4,128)} fusion(f32[16,40,2,4,256]{4,3,2,1,0:T(4,128)} %shard_map.126, f32[40,2,4,256]{3,2,1,0:T(4,128)S(1)} %fusion.3, f32[40]{0:T(128)S(1)} %copy-done.4), kind=kLoop, calls=%fused_computation | loop fusion | flops 3932160 | bytes 10813600 | tf_op jit(solution)/shard_map/add | solution.py:557
  (51 shorter events, 0.9 us)
Async XLA Ops:
  9.9 4.2 %copy-start.5 = (s32[128]{0:T(128)}, s32[128]{0:T(128)S(1)}, u32[]{:S(2)}) copy-start(s32[128]{0:T(128)S(1)} %select_reduce_fusion.1.order_ref) | copy-start | bytes 1540
  141.2 39.1 %copy-start.2 = (f32[40]{0:T(128)S(1)}, f32[40]{0:T(128)}, u32[]{:S(2)}) copy-start(f32[40]{0:T(128)} %param.18) | copy-start | bytes 484
  182.7 2.1 copy-start
  202.4 144.3 %copy-start.3 = (f32[40]{0:T(128)S(1)}, f32[40]{0:T(128)}, u32[]{:S(2)}) copy-start(f32[40]{0:T(128)} %param.17) | copy-start | bytes 484
  321.8 25.3 %copy-start.4 = (f32[40]{0:T(128)S(1)}, f32[40]{0:T(128)}, u32[]{:S(2)}) copy-start(f32[40]{0:T(128)} %param.16) | copy-start | bytes 484
  346.7 6.6 %copy-start.1 = (f32[2,4,256]{2,1,0:T(4,128)}, f32[2,4,256]{2,1,0:T(4,128)S(1)}, u32[]{:S(2)}) copy-start(f32[2,4,256]{2,1,0:T(4,128)S(1)} %maximum_minimum_fusion.3) | copy-start | bytes 24580

commit v3 on v2

v3 whole, which is shorter than its diff:
```python
import functools

import jax
import jax.numpy as jnp
from jax import lax
from jax.experimental import pallas as pl
from jax.experimental.pallas import tpu as pltpu
from jax.sharding import PartitionSpec as P

NEWTON = 4
BLOCK = 128
OCT = 8


def pick(values, index):
    hits = index[:, None] == jnp.arange(values.shape[0], dtype=jnp.int32)[None, :]
    return jnp.sum(jnp.where(hits, values[None, :], jnp.zeros((), values.dtype)), axis=1)


def orbit_order(directions, mirror):
    count = directions.shape[1]
    ids = jnp.arange(count, dtype=jnp.int32)
    positive = (directions > 0).astype(jnp.int32)
    code = positive[0] + 2 * positive[1] + 4 * positive[2]
    rep = ids
    for axis_num in range(3):
        flipped = pick(mirror[axis_num], rep)
        rep = jnp.where(positive[axis_num] > 0, rep, flipped)
    is_rep = code == 7
    rank_of_rep = jnp.sum(
        jnp.where(is_rep[None, :] & (ids[None, :] < rep[:, None]), 1, 0), axis=1
    ).astype(jnp.int32)
    position = rank_of_rep * OCT + code
    order = jnp.sum(
        jnp.where(position[None, :] == ids[:, None], ids[None, :], 0), axis=1
    ).astype(jnp.int32)
    return order, position


def facet_grid(wall_blocks, wall_count, wall_facet, tile_blocks):
    slot_ids = jnp.arange(wall_blocks.shape[0], dtype=jnp.int32)
    hits = (wall_blocks[None, :] == jnp.arange(tile_blocks, dtype=jnp.int32)[:, None]) & (
        slot_ids < wall_count
    )[None, :]
    return jnp.sum(jnp.where(hits[:, :, None], wall_facet[None], 0), axis=1).astype(jnp.int32)


def roll(u, by, axis):
    return pltpu.roll(u, by % u.shape[axis], axis)


def sweep_unit(high, tiles, coef_ref, unit, facets_ref, load, store):
    coef = [coef_ref[unit, i] for i in range(10)]
    _, rows, width = facets_ref.shape
    row_id = lax.broadcasted_iota(jnp.int32, (rows, width), 0)
    height = row_id % high
    total = [jnp.zeros((rows, width), jnp.float32) for _ in range(tiles)]
    for o in range(OCT):
        way = [1 if o >> a & 1 else -1 for a in range(3)]
        cells = []
        for t in range(tiles):
            facets = facets_ref[t]
            u = load(t, o)
            for a in range(3):
                facing = float(2 * a + 1 if way[a] > 0 else 2 * a + 2)
                u = jnp.where(facets == facing, load(t, o ^ (1 << a)), u)
            cells.append(u)
        turned = [roll(u, high * way[0], 0) for u in cells]
        for t in range(tiles):
            up = (t - way[0]) % tiles
            edge = row_id < high if way[0] > 0 else row_id >= rows - high
            near = jnp.where(edge, turned[up], turned[t])
            u = coef[0] * cells[t] + coef[1] * near + coef[2] * cells[up]
            u = coef[3] * u + coef[4] * roll(u, way[1], 1) + coef[5] * roll(u, 2 * way[1], 1)
            wrap1 = height < 1 if way[2] > 0 else height >= high - 1
            wrap2 = height < 2 if way[2] > 0 else height >= high - 2
            near = jnp.where(wrap1, roll(u, (1 - high) * way[2], 0), roll(u, way[2], 0))
            far = jnp.where(wrap2, roll(u, (2 - high) * way[2], 0), roll(u, 2 * way[2], 0))
            u = coef[6] * u + coef[7] * near + coef[8] * far
            store(t, o, u)
            total[t] = total[t] + u
    return [coef[9] * total[t] for t in range(tiles)]


MESH = pl.DeviceIdType.MESH


def greet(tile, tiles, group, groups):
    barrier = pltpu.get_barrier_semaphore()
    for u in range(1, tiles):
        pl.semaphore_signal(
            barrier, inc=1, device_id=(lax.rem(tile + u, tiles), group), device_id_type=MESH
        )
    for t in range(1, groups):
        pl.semaphore_signal(
            barrier, inc=1, device_id=(tile, lax.rem(group + t, groups)), device_id_type=MESH
        )
    pl.semaphore_wait(barrier, tiles + groups - 2)


def remote(src, dst, send, recv, device):
    return pltpu.make_async_remote_copy(
        src_ref=src, dst_ref=dst, send_sem=send, recv_sem=recv, device_id=device, device_id_type=MESH
    )


CUTS = 2


def spread_kernel(
    tiles, groups, order_ref, coef_ref, facet_ref, home_ref, moved_ref, source_ref, facets_ref, *scratch
):
    _, part, share, rows, deep = moved_ref.shape
    chunks = share * CUTS
    width = deep // CUTS
    landed, sorted_refs = scratch[:chunks], scratch[chunks : 2 * chunks]
    fields = scratch[2 * chunks : 2 * chunks + share]
    dir_send, dir_recv, tile_send, tile_recv, facet_send, facet_recv, own_sem = scratch[
        2 * chunks + share :
    ]
    local_dirs, _, wide, high, _ = home_ref.shape
    dirs, orbits = landed[0].shape[0], part // OCT
    tile, group = lax.axis_index("space"), lax.axis_index("dir")

    def lanes(c):
        return pl.ds(c % CUTS * width, width)

    own = [
        pltpu.make_async_copy(
            home_ref.at[:, group * share + c // CUTS, :, :, lanes(c)],
            landed[c].at[pl.ds(group * local_dirs, local_dirs)],
            own_sem.at[c],
        )
        for c in range(chunks)
    ]
    for copy in own:
        copy.start()
    own_facets = pltpu.make_async_copy(facet_ref, facets_ref.at[tile], own_sem.at[2 * chunks])
    own_facets.start()
    greet(tile, tiles, group, groups)

    third = []
    for u in range(1, tiles):
        copy = remote(
            facet_ref,
            facets_ref.at[tile],
            facet_send.at[u],
            facet_recv.at[u],
            (lax.rem(tile + u, tiles), group),
        )
        copy.start()
        third.append(copy)
    first = []
    for c in range(chunks):
        line = []
        for t in range(1, groups):
            peer = lax.rem(group + t, groups)
            copy = remote(
                home_ref.at[:, peer * share + c // CUTS, :, :, lanes(c)],
                landed[c].at[pl.ds(group * local_dirs, local_dirs)],
                dir_send.at[c, t],
                dir_recv.at[c, t],
                (tile, peer),
            )
            copy.start()
            line.append(copy)
        first.append(line)

    second = []
    source_ref[...] = jnp.zeros_like(source_ref)

    def sweep_band(k):
        for c in range(k * CUTS, (k + 1) * CUTS):
            second[c][0].wait()
            for copy in second[c][1:]:
                copy.wait_recv()

        def one(orbit, carry):
            def store(t, o, u):
                moved_ref[t, orbit * OCT + o, k] = u

            sums = sweep_unit(
                high,
                tiles,
                coef_ref,
                k * orbits + orbit,
                facets_ref,
                lambda t, o: fields[k][t, orbit * OCT + o],
                store,
            )
            for t in range(tiles):
                source_ref[t] = source_ref[t] + sums[t]
            return carry

        lax.fori_loop(0, orbits, one, 0)

    for c in range(chunks):
        own[c].wait()
        for copy in first[c]:
            copy.wait_recv()

        def move(j, carry):
            d = order_ref[j]
            for x in range(wide):
                sorted_refs[c][j, x * high : (x + 1) * high, :] = landed[c][d, x]
            return carry

        lax.fori_loop(0, dirs, move, 0, unroll=4)
        line = [
            pltpu.make_async_copy(
                sorted_refs[c].at[pl.ds(tile * part, part)],
                fields[c // CUTS].at[tile, :, :, lanes(c)],
                own_sem.at[chunks + c],
            )
        ]
        for u in range(1, tiles):
            peer = lax.rem(tile + u, tiles)
            line.append(
                remote(
                    sorted_refs[c].at[pl.ds(peer * part, part)],
                    fields[c // CUTS].at[tile, :, :, lanes(c)],
                    tile_send.at[c, u],
                    tile_recv.at[c, u],
                    (peer, group),
                )
            )
        for copy in line:
            copy.start()
        second.append(line)
        if c == 0:
            own_facets.wait()
            for copy in third:
                copy.wait_recv()
        if c >= CUTS and c % CUTS == 0:
            sweep_band(c // CUTS - 1)
    sweep_band(share - 1)
    for line in first:
        for copy in line:
            copy.wait_send()
    for line in second:
        for copy in line[1:]:
            copy.wait_send()
    for copy in third:
        copy.wait_send()


def spread(tiles, groups, share, order, coefs, facets, home):
    local_dirs, _, wide, high, deep = home.shape
    dirs, rows = local_dirs * groups, wide * high
    part = dirs // tiles
    chunks, width = share * CUTS, deep // CUTS
    vmem = pl.BlockSpec(memory_space=pltpu.VMEM)
    smem = pl.BlockSpec(memory_space=pltpu.SMEM)
    dma = pltpu.SemaphoreType.DMA
    return pl.pallas_call(
        functools.partial(spread_kernel, tiles, groups),
        in_specs=[smem, smem, vmem, pl.BlockSpec(memory_space=pl.ANY)],
        out_specs=[vmem, vmem, vmem],
        out_shape=[
            jax.ShapeDtypeStruct((tiles, part, share, rows, deep), jnp.float32),
            jax.ShapeDtypeStruct((tiles, rows, deep), jnp.float32),
            jax.ShapeDtypeStruct((tiles, rows, deep), jnp.float32),
        ],
        scratch_shapes=[pltpu.VMEM((dirs, wide, high, width), jnp.float32)] * chunks
        + [pltpu.VMEM((dirs, rows, width), jnp.float32)] * chunks
        + [pltpu.VMEM((tiles, part, rows, deep), jnp.float32)] * share
        + [
            dma((chunks, groups)),
            dma((chunks, groups)),
            dma((chunks, tiles)),
            dma((chunks, tiles)),
            dma((tiles,)),
            dma((tiles,)),
            dma((2 * chunks + 1,)),
        ],
        compiler_params=pltpu.CompilerParams(collective_id=0, has_side_effects=True),
    )(order, coefs, facets, home)


def collect_kernel(
    tiles, groups, position_ref, coef_ref, facets_ref, field_ref, bose_ref, home_ref, total_ref, *scratch
):
    _, part, share, rows, deep = field_ref.shape
    chunks = share * CUTS
    width = deep // CUTS
    landed, sorted_refs = scratch[:chunks], scratch[chunks : 2 * chunks]
    swept = scratch[2 * chunks : 2 * chunks + share]
    now_ref, source_ref, near, summed, far = scratch[2 * chunks + share : 2 * chunks + share + 5]
    dir_send, dir_recv, tile_send, tile_recv, near_send, near_recv, far_send, far_recv, own_sem = (
        scratch[2 * chunks + share + 5 :]
    )
    local_dirs, _, wide, high, _ = home_ref.shape
    dirs, orbits = part * tiles, part // OCT
    tile, group = lax.axis_index("space"), lax.axis_index("dir")
    greet(tile, tiles, group, groups)
    source_ref[...] = jnp.zeros_like(source_ref)
    first = []
    for k in range(share):

        def one(orbit, carry):
            unit = k * orbits + orbit
            for t in range(tiles):
                bose = bose_ref[k, t]
                for o in range(OCT):
                    u = field_ref[t, orbit * OCT + o, k]
                    now_ref[t, o] = u + coef_ref[unit, 10] * (bose - u)

            def store(t, o, u):
                swept[k][t, orbit * OCT + o] = u

            sums = sweep_unit(
                high, tiles, coef_ref, unit, facets_ref, lambda t, o: now_ref[t, o], store
            )
            for t in range(tiles):
                source_ref[t] = source_ref[t] + sums[t]
            return carry

        lax.fori_loop(0, orbits, one, 0)
        for c in range(k * CUTS, (k + 1) * CUTS):
            lanes = pl.ds(c % CUTS * width, width)
            line = [
                pltpu.make_async_copy(
                    swept[k].at[tile, :, :, lanes],
                    landed[c].at[pl.ds(tile * part, part)],
                    own_sem.at[c],
                )
            ]
            for u in range(1, tiles):
                peer = lax.rem(tile + u, tiles)
                line.append(
                    remote(
                        swept[k].at[peer, :, :, lanes],
                        landed[c].at[pl.ds(tile * part, part)],
                        tile_send.at[c, u],
                        tile_recv.at[c, u],
                        (peer, group),
                    )
                )
            for copy in line:
                copy.start()
            first.append(line)
    nears = []
    for u in range(1, tiles):
        peer = lax.rem(tile + u, tiles)
        copy = remote(
            source_ref.at[peer], near.at[u], near_send.at[u], near_recv.at[u], (peer, group)
        )
        copy.start()
        nears.append(copy)
    second, fars = [], []
    for c in range(chunks):
        first[c][0].wait()
        for copy in first[c][1:]:
            copy.wait_recv()

        def move(d, carry):
            j = position_ref[d]
            for x in range(wide):
                sorted_refs[c][d, x] = landed[c][j, x * high : (x + 1) * high, :]
            return carry

        lax.fori_loop(0, dirs, move, 0, unroll=4)
        lanes = pl.ds(c % CUTS * width, width)
        line = [
            pltpu.make_async_copy(
                sorted_refs[c].at[pl.ds(group * local_dirs, local_dirs)],
                home_ref.at[:, group * share + c // CUTS, :, :, lanes],
                own_sem.at[chunks + c],
            )
        ]
        for t in range(1, groups):
            peer = lax.rem(group + t, groups)
            line.append(
                remote(
                    sorted_refs[c].at[pl.ds(peer * local_dirs, local_dirs)],
                    home_ref.at[:, group * share + c // CUTS, :, :, lanes],
                    dir_send.at[c, t],
                    dir_recv.at[c, t],
                    (tile, peer),
                )
            )
        for copy in line:
            copy.start()
        second.append(line)
        if c == chunks - 1:
            value = source_ref[tile]
            for u in range(1, tiles):
                nears[u - 1].wait_recv()
                value = value + near[u]
            summed[...] = value
            for t in range(1, groups):
                peer = lax.rem(group + t, groups)
                copy = remote(summed, far.at[group], far_send.at[t], far_recv.at[t], (tile, peer))
                copy.start()
                fars.append(copy)
            far[group] = value
    for line in second:
        line[0].wait()
        for copy in line[1:]:
            copy.wait_recv()
    for copy in fars:
        copy.wait_recv()
    value = far[0]
    for g in range(1, groups):
        value = value + far[g]
    total_ref[...] = value
    for line in first + second:
        for copy in line[1:]:
            copy.wait_send()
    for copy in nears + fars:
        copy.wait_send()


def collect(tiles, groups, position, coefs, facets, field, bose, high):
    _, part, share, rows, deep = field.shape
    dirs = part * tiles
    local_dirs, wide = dirs // groups, rows // high
    chunks, width = share * CUTS, deep // CUTS
    vmem = pl.BlockSpec(memory_space=pltpu.VMEM)
    smem = pl.BlockSpec(memory_space=pltpu.SMEM)
    dma = pltpu.SemaphoreType.DMA
    return pl.pallas_call(
        functools.partial(collect_kernel, tiles, groups),
        in_specs=[smem, smem, vmem, vmem, vmem],
        out_specs=[pl.BlockSpec(memory_space=pl.ANY), vmem],
        out_shape=[
            jax.ShapeDtypeStruct((local_dirs, share * groups, wide, high, deep), jnp.float32),
            jax.ShapeDtypeStruct((rows, deep), jnp.float32),
        ],
        scratch_shapes=[pltpu.VMEM((dirs, rows, width), jnp.float32)] * chunks
        + [pltpu.VMEM((dirs, wide, high, width), jnp.float32)] * chunks
        + [pltpu.VMEM((tiles, part, rows, deep), jnp.float32)] * share
        + [
            pltpu.VMEM((tiles, OCT, rows, deep), jnp.float32),
            pltpu.VMEM((tiles, rows, deep), jnp.float32),
            pltpu.VMEM((tiles, rows, deep), jnp.float32),
            pltpu.VMEM((rows, deep), jnp.float32),
            pltpu.VMEM((groups, rows, deep), jnp.float32),
            dma((chunks, groups)),
            dma((chunks, groups)),
            dma((chunks, tiles)),
            dma((chunks, tiles)),
            dma((tiles,)),
            dma((tiles,)),
            dma((groups,)),
            dma((groups,)),
            dma((2 * chunks,)),
        ],
        compiler_params=pltpu.CompilerParams(collective_id=1, has_side_effects=True),
    )(position, coefs, facets, field, bose)


def total_kernel(tiles, groups, part_ref, total_ref, near, own, far, summed, *sems):
    near_send, near_recv, far_send, far_recv, last_send, last_recv = sems
    tile, group = lax.axis_index("space"), lax.axis_index("dir")
    greet(tile, tiles, group, groups)
    copies = []
    for u in range(1, tiles):
        peer = lax.rem(tile + u, tiles)
        copy = remote(
            part_ref.at[peer], near.at[u], near_send.at[u], near_recv.at[u], (peer, group)
        )
        copy.start()
        copies.append(copy)
    value = part_ref[tile]
    for u in range(1, tiles):
        copies[u - 1].wait_recv()
        value = value + near[u]
    own[...] = value
    gathers = []
    for t in range(1, groups):
        peer = lax.rem(group + t, groups)
        copy = remote(own, far.at[group], far_send.at[t], far_recv.at[t], (tile, peer))
        copy.start()
        gathers.append(copy)
    far[group] = value
    for copy in gathers:
        copy.wait_recv()
    value = far[0]
    for g in range(1, groups):
        value = value + far[g]
    lasts = []
    summed[...] = value
    for u in range(1, tiles):
        peer = lax.rem(tile + u, tiles)
        copy = remote(summed, total_ref.at[tile], last_send.at[u], last_recv.at[u], (peer, group))
        copy.start()
        lasts.append(copy)
    total_ref[tile] = value
    for copy in lasts:
        copy.wait_recv()
    for copy in copies + gathers + lasts:
        copy.wait_send()


def total(tiles, groups, source):
    _, rows, deep = source.shape
    vmem = pl.BlockSpec(memory_space=pltpu.VMEM)
    dma = pltpu.SemaphoreType.DMA
    return pl.pallas_call(
        functools.partial(total_kernel, tiles, groups),
        in_specs=[vmem],
        out_specs=vmem,
        out_shape=jax.ShapeDtypeStruct((tiles, rows, deep), jnp.float32),
        scratch_shapes=[
            pltpu.VMEM((tiles, rows, deep), jnp.float32),
            pltpu.VMEM((rows, deep), jnp.float32),
            pltpu.VMEM((groups, rows, deep), jnp.float32),
            pltpu.VMEM((rows, deep), jnp.float32),
            dma((tiles,)),
            dma((tiles,)),
            dma((groups,)),
            dma((groups,)),
            dma((tiles,)),
            dma((tiles,)),
        ],
        compiler_params=pltpu.CompilerParams(
            collective_id=2, has_side_effects=True
        ),
    )(source)


def beam_coeffs(abs_speed):
    return (
        1.0 - 1.5 * abs_speed + 0.5 * abs_speed * abs_speed,
        2.0 * abs_speed - abs_speed * abs_speed,
        0.5 * abs_speed * abs_speed - 0.5 * abs_speed,
    )


def root_finder_guess(injection_contribution, collision_speed_factor, mode_pulsation):
    pseudo_kelvin_field = jnp.ones_like(injection_contribution)
    for newton_turn in range(NEWTON):
        dimensionless_pulsation = mode_pulsation[:, None] / pseudo_kelvin_field[None, :]
        heat_surplus = jnp.expm1(dimensionless_pulsation)
        mismatch_error = (
            jnp.sum(collision_speed_factor[:, None] / heat_surplus, axis=0) - injection_contribution
        )
        gradient_guess = (
            jnp.sum(
                collision_speed_factor[:, None]
                * dimensionless_pulsation
                * jnp.exp(dimensionless_pulsation)
                / (heat_surplus * heat_surplus),
                axis=0,
            )
            / pseudo_kelvin_field
        )
        pseudo_kelvin_field = jnp.clip(
            pseudo_kelvin_field - mismatch_error / gradient_guess,
            0.5 * pseudo_kelvin_field,
            2.0 * pseudo_kelvin_field,
        )
    return pseudo_kelvin_field


def on_device(
    phonon_heat_density,
    directions,
    quad_weight,
    mirror,
    band_courant,
    relax_rate,
    mode_heat_magnitude,
    mode_pulsation,
    wall_blocks,
    wall_count,
    wall_facet,
):
    local_dirs, bands, wide, high, deep = phonon_heat_density.shape
    tiles, groups = lax.axis_size("space"), lax.axis_size("dir")
    tile, group = lax.axis_index("space"), lax.axis_index("dir")
    rows = wide * high
    share = -(-bands // groups)
    extra = share * groups - bands
    dirs = directions.shape[1]
    orbits = dirs // OCT
    part = dirs // tiles
    part_orbits = orbits // tiles

    order, position = orbit_order(directions, mirror)
    own_facets = facet_grid(
        wall_blocks[0], wall_count[0], wall_facet[0], wide * high * deep // BLOCK
    ).astype(jnp.float32)
    def own_bands(values):
        return lax.dynamic_slice_in_dim(jnp.pad(values, (0, extra)), group * share, share)

    courant, rates = own_bands(band_courant), own_bands(relax_rate)
    magnitudes = own_bands(mode_heat_magnitude)
    pulsations = lax.dynamic_slice_in_dim(
        jnp.pad(mode_pulsation, (0, extra), constant_values=1.0), group * share, share
    )
    reps = lax.dynamic_slice_in_dim(
        order.reshape(orbits, OCT)[:, OCT - 1], tile * part_orbits, part_orbits
    )
    columns = []
    for axis_num in range(3):
        unit = jnp.abs(pick(directions[axis_num], reps))
        columns.extend(beam_coeffs(courant[:, None] * unit[None, :]))
    columns.append(rates[:, None] * pick(quad_weight, reps)[None, :])
    columns.append(jnp.broadcast_to(rates[:, None], columns[0].shape))
    coefs = jnp.stack(columns, axis=-1).reshape(share * part_orbits, len(columns))

    home = phonon_heat_density
    if extra:
        home = jnp.pad(home, ((0, 0), (0, extra), (0, 0), (0, 0), (0, 0)))
    field, source, facets = spread(
        tiles, groups, share, order, coefs, own_facets.reshape(rows, deep), home
    )
    collision_speed_factor = relax_rate * mode_heat_magnitude
    source = total(tiles, groups, source)
    kelvin = root_finder_guess(source.reshape(-1), collision_speed_factor, mode_pulsation)
    bose = magnitudes[:, None, None, None] / jnp.expm1(
        pulsations[:, None, None, None] / kelvin.reshape((1,) + source.shape)
    )
    moved, source = collect(tiles, groups, position, coefs, facets, field, bose, high)
    kelvin = root_finder_guess(source.reshape(-1), collision_speed_factor, mode_pulsation)
    kelvin = kelvin.reshape(wide, high, deep)
    moved = moved[:, :bands]
    home = mode_heat_magnitude[:, None, None, None] / jnp.expm1(
        mode_pulsation[:, None, None, None] / kelvin[None]
    )
    out = moved + relax_rate[None, :, None, None, None] * (home[None] - moved)
    return out, kelvin


def solution(mesh):
    in_specs = (
        P("dir", None, "space", None, None),
        P(),
        P(),
        P(),
        P(),
        P(),
        P(),
        P(),
        P("space", None),
        P("space"),
        P("space", None, None),
    )
    out_specs = (P("dir", None, "space", None, None), P("space", None, None))
    return jax.shard_map(
        on_device, mesh=mesh, in_specs=in_specs, out_specs=out_specs, check_vma=False
    )
```

time: 355 us -> 314 us (0.88)
  Pallas kernels: 316 us -> 277 us
    pallas_call x4 -> x1, Pallas kernels: 71.2 us -> 17 us  [total(): pl.pallas_call(functools.partial(total_kernel, tiles, groups), in_specs=[...]
    pallas_call x1, Pallas kernels: 119 us -> 131 us  [collect(): pl.pallas_call(functools.partial(collect_kernel, tiles, groups), in_specs...]
    pallas_call x1, Pallas kernels: 126 us -> 129 us  [spread(): pl.pallas_call(functools.partial(spread_kernel, tiles, groups), in_specs=...]
where the time goes in v3:
time: 314 us; the launch traced here: 313 us
  Pallas kernels  277 us (88%)
  other arithmetic  24.3 us (8%)
  local copies, waits for them, and re-layouts  9.22 us (3%)
    pallas_call x1, Pallas kernels, collect(): pl.pallas_call(functools.partial(collect_kernel, tiles, groups), in_specs...  131 us
    pallas_call x1, Pallas kernels, spread(): pl.pallas_call(functools.partial(spread_kernel, tiles, groups), in_specs=...  129 us
    pallas_call x1, Pallas kernels, total(): pl.pallas_call(functools.partial(total_kernel, tiles, groups), in_specs=[...  17 us
    min x8, other arithmetic, root_finder_guess(): jnp.clip(pseudo_kelvin_field - mismatch_error / gradient_guess, 0.5 * pse...  7.3 us
    add x1, other arithmetic, on_device(): out = moved + relax_rate[None, :, None, None, None] * (home[None] - moved)  6.28 us

profile of v3, /device:TPU:0, one launch (start us, length us, event | category | flops | bytes accessed | tf_op | source)
XLA Modules:
  0.0 312.5 jit_solution(3516094863070867243)
XLA Ops:
  1.3 0.7 dynamic_slice.15
  2.0 0.7 dynamic_slice.17
  2.8 0.7 dynamic_slice.18
  3.5 0.7 dynamic_slice.19
  4.2 0.7 fusion.12
  4.9 0.8 slice_bitcast_fusion.3
  5.7 0.1 select_reduce_fusion.5
  5.8 0.8 slice_bitcast_fusion.2
  6.6 1.3 divide_reduce_fusion.6
  7.9 0.7 compare_convert_fusion
  8.6 0.2 select_reduce_fusion.4
  8.8 0.2 select_reduce_fusion.3
  9.0 0.2 select_reduce_fusion.2
  9.2 0.5 bitcast_add_fusion.1.position_ref
  9.7 0.1 select_reduce_fusion.1.order_ref
  9.8 0.1 mul.649
  9.9 0.1 mul.650
  10.1 0.8 select_reduce_fusion
  10.9 0.6 convert_element_type.12.facet_ref
  11.6 0.1 reshape.704
  11.6 0.1 slice.43
  11.7 0.1 dynamic-slice_reduce_fusion
  11.8 0.9 select_reduce_fusion.6
  12.8 0.1 mul.652
  13.1 0.1 copy.50
  13.2 0.1 copy.49
  13.3 0.7 stack.2.coef_ref
  14.0 129.4 %shard_map.122 = (f32[4,32,5,8,256]{4,3,2,1,0:T(8,128)}, f32[4,8,256]{2,1,0:T(8,128)}, f32[4,8,256]{2,1,0:T(8,128)}) custom-call(s32[128]{0:T(128)} %copy-done.2, f32[20,11]{1,0:T(8,128)} %stack.2.coef_ref, f32[8,256]{1,0:T(8,128)} %convert_element_type.12.facet_ref, f32[16,40,2,4,256]{4,3,2,1,0:T(4,128)} %home_ref.1), custom_call_target="tpu_custom_call" | custom-call | tf_op jit(solution)/shard_map/pallas_call | solution.py:255
  143.4 17.0 %shard_map.123 = f32[4,8,256]{2,1,0:T(8,128)} custom-call(f32[4,8,256]{2,1,0:T(8,128)} %get-tuple-element.9.part_ref), custom_call_target="tpu_custom_call" | custom-call | tf_op jit(solution)/shard_map/pallas_call | solution.py:500
  160.4 0.8 copy.51
  161.2 1.2 subtract_clamp_fusion
  162.4 1.0 divide_reduce_fusion.2
  163.4 1.2 maximum_minimum_fusion.2
  164.7 1.0 divide_reduce_fusion.1
  165.8 1.0 divide_reduce_fusion
  166.8 1.2 maximum_minimum_fusion
  168.0 0.8 fusion.7.bose_ref
  168.9 130.9 %shard_map.124 = (f32[16,40,2,4,256]{4,3,2,1,0:T(4,128)}, f32[8,256]{1,0:T(8,128)}) custom-call(s32[128]{0:T(128)} %bitcast_add_fusion.1.position_ref, f32[20,11]{1,0:T(8,128)} %stack.2.coef_ref, f32[4,8,256]{2,1,0:T(8,128)} %get-tuple-element.7.facets_ref, f32[4,32,5,8,256]{4,3,2,1,0:T(8,128)} %get-tuple-element.8.field_ref, f32[5,4,8,256]{3,2,1,0:T(8,128)} %fusion.7.bose_ref), custom_call_target="tpu_custom_call" | custom-call | tf_op jit(solution)/shard_map/pallas_call | solution.py:422
  299.8 0.7 copy.52
  300.5 1.2 subtract_clamp_fusion.1
  301.7 0.7 reshape.706
  302.4 0.3 divide_reduce_fusion.5
  302.7 1.2 maximum_minimum_fusion.5
  303.9 0.3 divide_reduce_fusion.4
  304.3 0.3 divide_reduce_fusion.3
  304.6 1.2 maximum_minimum_fusion.3
  305.9 0.3 fusion.3
  306.2 6.3 %multiply_add_fusion = f32[16,40,2,4,256]{4,3,2,1,0:T(4,128)} fusion(f32[16,40,2,4,256]{4,3,2,1,0:T(4,128)} %get-tuple-element.10, f32[40,2,4,256]{3,2,1,0:T(4,128)S(1)} %fusion.3, f32[40]{0:T(128)S(1)} %copy-done.5), kind=kLoop, calls=%fused_computation | loop fusion | flops 3932160 | bytes 10813600 | tf_op jit(solution)/shard_map/add | solution.py:623
  (47 shorter events, 0.6 us)
Async XLA Ops:
  9.8 4.2 %copy-start.2 = (s32[128]{0:T(128)}, s32[128]{0:T(128)S(1)}, u32[]{:S(2)}) copy-start(s32[128]{0:T(128)S(1)} %select_reduce_fusion.1.order_ref) | copy-start | bytes 1540
  14.0 148.4 %copy-start.3 = (f32[40]{0:T(128)S(1)}, f32[40]{0:T(128)}, u32[]{:S(2)}) copy-start(f32[40]{0:T(128)} %param.18) | copy-start | bytes 484
  164.7 2.1 copy-start
  168.9 137.0 %copy-start.4 = (f32[40]{0:T(128)S(1)}, f32[40]{0:T(128)}, u32[]{:S(2)}) copy-start(f32[40]{0:T(128)} %param.17) | copy-start | bytes 484
  299.8 6.4 %copy-start.5 = (f32[40]{0:T(128)S(1)}, f32[40]{0:T(128)}, u32[]{:S(2)}) copy-start(f32[40]{0:T(128)} %param.16) | copy-start | bytes 484
  305.9 6.6 %copy-start.1 = (f32[2,4,256]{2,1,0:T(4,128)}, f32[2,4,256]{2,1,0:T(4,128)S(1)}, u32[]{:S(2)}) copy-start(f32[2,4,256]{2,1,0:T(4,128)S(1)} %maximum_minimum_fusion.3) | copy-start | bytes 24580

commit v4 on v3

--- a/solution.py
+++ b/solution.py
@@ -49,8 +49,49 @@
     return pltpu.roll(u, by % u.shape[axis], axis)
 
 
-def sweep_unit(high, tiles, coef_ref, unit, facets_ref, load, store):
-    coef = [coef_ref[unit, i] for i in range(10)]
+def unit_coeffs(scalars, band, orbit):
+    order_ref, directions_ref, weight_ref, courant_ref, rate_ref = scalars
+    bands = courant_ref.shape[0]
+    real = band < bands
+    index = jnp.minimum(band, bands - 1)
+    courant, rate = courant_ref[index], jnp.where(real, rate_ref[index], 0.0)
+    rep = order_ref[orbit * OCT + OCT - 1]
+    coef = []
+    for axis_num in range(3):
+        coef.extend(beam_coeffs(courant * jnp.abs(directions_ref[axis_num, rep])))
+    coef.append(rate * weight_ref[rep])
+    return coef, rate
+
+
+def surplus_of(q):
+    series = jnp.ones_like(q)
+    for n in range(9, 1, -1):
+        series = 1.0 + series * (q * (1.0 / n))
+    return jnp.where(q < 0.5, q * series, jnp.exp(q) - 1.0)
+
+
+def newton(rate_ref, magnitude_ref, pulsation_ref, source):
+    kelvin = jnp.ones_like(source)
+    for newton_turn in range(NEWTON):
+        inverse = 1.0 / kelvin
+
+        def one(b, carry):
+            mismatch, gradient = carry
+            factor = rate_ref[b] * magnitude_ref[b]
+            q = pulsation_ref[b] * inverse
+            surplus = surplus_of(q)
+            ratio = 1.0 / surplus
+            term = factor * ratio
+            return mismatch + term, gradient + term * q * ((surplus + 1.0) * ratio)
+
+        zero = jnp.zeros_like(source)
+        mismatch, gradient = lax.fori_loop(0, rate_ref.shape[0], one, (zero, zero), unroll=8)
+        mismatch, gradient = mismatch - source, gradient * inverse
+        kelvin = jnp.clip(kelvin - mismatch / gradient, 0.5 * kelvin, 2.0 * kelvin)
+    return kelvin
+
+
+def sweep_unit(high, tiles, coef, facets_ref, load, store):
     _, rows, width = facets_ref.shape
     row_id = lax.broadcasted_iota(jnp.int32, (rows, width), 0)
     height = row_id % high
@@ -108,15 +149,21 @@
 
 
 def spread_kernel(
-    tiles, groups, order_ref, coef_ref, facet_ref, home_ref, moved_ref, source_ref, facets_ref, *scratch
+    tiles, groups, order_ref, directions_ref, weight_ref, courant_ref, rate_ref, magnitude_ref,
+    pulsation_ref, facet_ref, home_ref, moved_ref, kelvin_ref, facets_ref, *scratch
 ):
+    scalars = (order_ref, directions_ref, weight_ref, courant_ref, rate_ref)
     _, part, share, rows, deep = moved_ref.shape
     chunks = share * CUTS
     width = deep // CUTS
     landed, sorted_refs = scratch[:chunks], scratch[chunks : 2 * chunks]
     fields = scratch[2 * chunks : 2 * chunks + share]
+    source_ref, near, summed, far, found = scratch[2 * chunks + share : 2 * chunks + share + 5]
     dir_send, dir_recv, tile_send, tile_recv, facet_send, facet_recv, own_sem = scratch[
-        2 * chunks + share :
+        2 * chunks + share + 5 : 2 * chunks + share + 12
+    ]
+    near_send, near_recv, far_send, far_recv, last_send, last_recv = scratch[
+        2 * chunks + share + 12 :
     ]
     local_dirs, _, wide, high, _ = home_ref.shape
     dirs, orbits = landed[0].shape[0], part // OCT
@@ -179,11 +226,11 @@
             def store(t, o, u):
                 moved_ref[t, orbit * OCT + o, k] = u
 
+            coef, _ = unit_coeffs(scalars, group * share + k, tile * orbits + orbit)
             sums = sweep_unit(
                 high,
                 tiles,
-                coef_ref,
-                k * orbits + orbit,
+                coef,
                 facets_ref,
                 lambda t, o: fields[k][t, orbit * OCT + o],
                 store,
@@ -234,6 +281,45 @@
         if c >= CUTS and c % CUTS == 0:
             sweep_band(c // CUTS - 1)
     sweep_band(share - 1)
+
+    copies = []
+    for u in range(1, tiles):
+        peer = lax.rem(tile + u, tiles)
+        copy = remote(
+            source_ref.at[peer], near.at[u], near_send.at[u], near_recv.at[u], (peer, group)
+        )
+        copy.start()
+        copies.append(copy)
+    value = source_ref[tile]
+    for u in range(1, tiles):
+        copies[u - 1].wait_recv()
+        value = value + near[u]
+    summed[...] = value
+    gathers = []
+    for t in range(1, groups):
+        peer = lax.rem(group + t, groups)
+        copy = remote(summed, far.at[group], far_send.at[t], far_recv.at[t], (tile, peer))
+        copy.start()
+        gathers.append(copy)
+    far[group] = value
+    for copy in gathers:
+        copy.wait_recv()
+    value = far[0]
+    for g in range(1, groups):
+        value = value + far[g]
+    value = newton(rate_ref, magnitude_ref, pulsation_ref, value)
+    found[...] = value
+    lasts = []
+    for u in range(1, tiles):
+        peer = lax.rem(tile + u, tiles)
+        copy = remote(found, kelvin_ref.at[tile], last_send.at[u], last_recv.at[u], (peer, group))
+        copy.start()
+        lasts.append(copy)
+    kelvin_ref[tile] = value
+    for copy in lasts:
+        copy.wait_recv()
+    for copy in copies + gathers + lasts:
+        copy.wait_send()
     for line in first:
         for copy in line:
             copy.wait_send()
@@ -244,7 +330,7 @@
         copy.wait_send()
 
 
-def spread(tiles, groups, share, order, coefs, facets, home):
+def spread(tiles, groups, share, scalars, facets, home):
     local_dirs, _, wide, high, deep = home.shape
     dirs, rows = local_dirs * groups, wide * high
     part = dirs // tiles
@@ -254,7 +340,7 @@
     dma = pltpu.SemaphoreType.DMA
     return pl.pallas_call(
         functools.partial(spread_kernel, tiles, groups),
-        in_specs=[smem, smem, vmem, pl.BlockSpec(memory_space=pl.ANY)],
+        in_specs=[smem] * len(scalars) + [vmem, pl.BlockSpec(memory_space=pl.ANY)],
         out_specs=[vmem, vmem, vmem],
         out_shape=[
             jax.ShapeDtypeStruct((tiles, part, share, rows, deep), jnp.float32),
@@ -265,6 +351,11 @@
         + [pltpu.VMEM((dirs, rows, width), jnp.float32)] * chunks
         + [pltpu.VMEM((tiles, part, rows, deep), jnp.float32)] * share
         + [
+            pltpu.VMEM((tiles, rows, deep), jnp.float32),
+            pltpu.VMEM((tiles, rows, deep), jnp.float32),
+            pltpu.VMEM((rows, deep), jnp.float32),
+            pltpu.VMEM((groups, rows, deep), jnp.float32),
+            pltpu.VMEM((rows, deep), jnp.float32),
             dma((chunks, groups)),
             dma((chunks, groups)),
             dma((chunks, tiles)),
@@ -272,22 +363,32 @@
             dma((tiles,)),
             dma((tiles,)),
             dma((2 * chunks + 1,)),
+            dma((tiles,)),
+            dma((tiles,)),
+            dma((groups,)),
+            dma((groups,)),
+            dma((tiles,)),
+            dma((tiles,)),
         ],
         compiler_params=pltpu.CompilerParams(collective_id=0, has_side_effects=True),
-    )(order, coefs, facets, home)
+    )(*scalars, facets, home)
 
 
 def collect_kernel(
-    tiles, groups, position_ref, coef_ref, facets_ref, field_ref, bose_ref, home_ref, total_ref, *scratch
+    tiles, groups, position_ref, order_ref, directions_ref, weight_ref, courant_ref, rate_ref,
+    magnitude_ref, pulsation_ref, facets_ref, field_ref, before_ref, home_ref, kelvin_ref, *scratch
 ):
+    scalars = (order_ref, directions_ref, weight_ref, courant_ref, rate_ref)
     _, part, share, rows, deep = field_ref.shape
     chunks = share * CUTS
     width = deep // CUTS
     landed, sorted_refs = scratch[:chunks], scratch[chunks : 2 * chunks]
     swept = scratch[2 * chunks : 2 * chunks + share]
-    now_ref, source_ref, near, summed, far = scratch[2 * chunks + share : 2 * chunks + share + 5]
+    now_ref, source_ref, near, summed, far, bose_ref = scratch[
+        2 * chunks + share : 2 * chunks + share + 6
+    ]
     dir_send, dir_recv, tile_send, tile_recv, near_send, near_recv, far_send, far_recv, own_sem = (
-        scratch[2 * chunks + share + 5 :]
+        scratch[2 * chunks + share + 6 :]
     )
     local_dirs, _, wide, high, _ = home_ref.shape
     dirs, orbits = part * tiles, part // OCT
@@ -296,20 +397,23 @@
     source_ref[...] = jnp.zeros_like(source_ref)
     first = []
     for k in range(share):
+        band = jnp.minimum(group * share + k, courant_ref.shape[0] - 1)
+        for t in range(tiles):
+            bose_ref[t] = magnitude_ref[band] / surplus_of(pulsation_ref[band] / before_ref[t])
 
         def one(orbit, carry):
-            unit = k * orbits + orbit
+            coef, rate = unit_coeffs(scalars, group * share + k, tile * orbits + orbit)
             for t in range(tiles):
-                bose = bose_ref[k, t]
+                bose = bose_ref[t]
                 for o in range(OCT):
                     u = field_ref[t, orbit * OCT + o, k]
-                    now_ref[t, o] = u + coef_ref[unit, 10] * (bose - u)
+                    now_ref[t, o] = u + rate * (bose - u)
 
             def store(t, o, u):
                 swept[k][t, orbit * OCT + o] = u
 
             sums = sweep_unit(
-                high, tiles, coef_ref, unit, facets_ref, lambda t, o: now_ref[t, o], store
+                high, tiles, coef, facets_ref, lambda t, o: now_ref[t, o], store
             )
             for t in range(tiles):
                 source_ref[t] = source_ref[t] + sums[t]
@@ -382,7 +486,7 @@
         for copy in line:
             copy.start()
         second.append(line)
-        if c == chunks - 1:
+        if c == chunks // 2 - 1:
             value = source_ref[tile]
             for u in range(1, tiles):
                 nears[u - 1].wait_recv()
@@ -394,16 +498,16 @@
                 copy.start()
                 fars.append(copy)
             far[group] = value
-    for line in second:
-        line[0].wait()
-        for copy in line[1:]:
-            copy.wait_recv()
     for copy in fars:
         copy.wait_recv()
     value = far[0]
     for g in range(1, groups):
         value = value + far[g]
-    total_ref[...] = value
+    kelvin_ref[...] = newton(rate_ref, magnitude_ref, pulsation_ref, value)
+    for line in second:
+        line[0].wait()
+        for copy in line[1:]:
+            copy.wait_recv()
     for line in first + second:
         for copy in line[1:]:
             copy.wait_send()
@@ -411,7 +515,7 @@
         copy.wait_send()
 
 
-def collect(tiles, groups, position, coefs, facets, field, bose, high):
+def collect(tiles, groups, position, scalars, facets, field, kelvin, high):
     _, part, share, rows, deep = field.shape
     dirs = part * tiles
     local_dirs, wide = dirs // groups, rows // high
@@ -421,7 +525,7 @@
     dma = pltpu.SemaphoreType.DMA
     return pl.pallas_call(
         functools.partial(collect_kernel, tiles, groups),
-        in_specs=[smem, smem, vmem, vmem, vmem],
+        in_specs=[smem] * (1 + len(scalars)) + [vmem, vmem, vmem],
         out_specs=[pl.BlockSpec(memory_space=pl.ANY), vmem],
         out_shape=[
             jax.ShapeDtypeStruct((local_dirs, share * groups, wide, high, deep), jnp.float32),
@@ -436,6 +540,7 @@
             pltpu.VMEM((tiles, rows, deep), jnp.float32),
             pltpu.VMEM((rows, deep), jnp.float32),
             pltpu.VMEM((groups, rows, deep), jnp.float32),
+            pltpu.VMEM((tiles, rows, deep), jnp.float32),
             dma((chunks, groups)),
             dma((chunks, groups)),
             dma((chunks, tiles)),
@@ -447,77 +552,7 @@
             dma((2 * chunks,)),
         ],
         compiler_params=pltpu.CompilerParams(collective_id=1, has_side_effects=True),
-    )(position, coefs, facets, field, bose)
-
-
-def total_kernel(tiles, groups, part_ref, total_ref, near, own, far, summed, *sems):
-    near_send, near_recv, far_send, far_recv, last_send, last_recv = sems
-    tile, group = lax.axis_index("space"), lax.axis_index("dir")
-    greet(tile, tiles, group, groups)
-    copies = []
-    for u in range(1, tiles):
-        peer = lax.rem(tile + u, tiles)
-        copy = remote(
-            part_ref.at[peer], near.at[u], near_send.at[u], near_recv.at[u], (peer, group)
-        )
-        copy.start()
-        copies.append(copy)
-    value = part_ref[tile]
-    for u in range(1, tiles):
-        copies[u - 1].wait_recv()
-        value = value + near[u]
-    own[...] = value
-    gathers = []
-    for t in range(1, groups):
-        peer = lax.rem(group + t, groups)
-        copy = remote(own, far.at[group], far_send.at[t], far_recv.at[t], (tile, peer))
-        copy.start()
-        gathers.append(copy)
-    far[group] = value
-    for copy in gathers:
-        copy.wait_recv()
-    value = far[0]
-    for g in range(1, groups):
-        value = value + far[g]
-    lasts = []
-    summed[...] = value
-    for u in range(1, tiles):
-        peer = lax.rem(tile + u, tiles)
-        copy = remote(summed, total_ref.at[tile], last_send.at[u], last_recv.at[u], (peer, group))
-        copy.start()
-        lasts.append(copy)
-    total_ref[tile] = value
-    for copy in lasts:
-        copy.wait_recv()
-    for copy in copies + gathers + lasts:
-        copy.wait_send()
-
-
-def total(tiles, groups, source):
-    _, rows, deep = source.shape
-    vmem = pl.BlockSpec(memory_space=pltpu.VMEM)
-    dma = pltpu.SemaphoreType.DMA
-    return pl.pallas_call(
-        functools.partial(total_kernel, tiles, groups),
-        in_specs=[vmem],
-        out_specs=vmem,
-        out_shape=jax.ShapeDtypeStruct((tiles, rows, deep), jnp.float32),
-        scratch_shapes=[
-            pltpu.VMEM((tiles, rows, deep), jnp.float32),
-            pltpu.VMEM((rows, deep), jnp.float32),
-            pltpu.VMEM((groups, rows, deep), jnp.float32),
-            pltpu.VMEM((rows, deep), jnp.float32),
-            dma((tiles,)),
-            dma((tiles,)),
-            dma((groups,)),
-            dma((groups,)),
-            dma((tiles,)),
-            dma((tiles,)),
-        ],
-        compiler_params=pltpu.CompilerParams(
-            collective_id=2, has_side_effects=True
-        ),
-    )(source)
+    )(position, *scalars, facets, field, kelvin)
 
 
 def beam_coeffs(abs_speed):
@@ -526,32 +561,6 @@
         2.0 * abs_speed - abs_speed * abs_speed,
         0.5 * abs_speed * abs_speed - 0.5 * abs_speed,
     )
-
-
-def root_finder_guess(injection_contribution, collision_speed_factor, mode_pulsation):
-    pseudo_kelvin_field = jnp.ones_like(injection_contribution)
-    for newton_turn in range(NEWTON):
-        dimensionless_pulsation = mode_pulsation[:, None] / pseudo_kelvin_field[None, :]
-        heat_surplus = jnp.expm1(dimensionless_pulsation)
-        mismatch_error = (
-            jnp.sum(collision_speed_factor[:, None] / heat_surplus, axis=0) - injection_contribution
-        )
-        gradient_guess = (
-            jnp.sum(
-                collision_speed_factor[:, None]
-                * dimensionless_pulsation
-                * jnp.exp(dimensionless_pulsation)
-                / (heat_surplus * heat_surplus),
-                axis=0,
-            )
-            / pseudo_kelvin_field
-        )
-        pseudo_kelvin_field = jnp.clip(
-            pseudo_kelvin_field - mismatch_error / gradient_guess,
-            0.5 * pseudo_kelvin_field,
-            2.0 * pseudo_kelvin_field,
-        )
-    return pseudo_kelvin_field
 
 
 def on_device(
@@ -569,52 +578,30 @@
 ):
     local_dirs, bands, wide, high, deep = phonon_heat_density.shape
     tiles, groups = lax.axis_size("space"), lax.axis_size("dir")
-    tile, group = lax.axis_index("space"), lax.axis_index("dir")
     rows = wide * high
     share = -(-bands // groups)
     extra = share * groups - bands
-    dirs = directions.shape[1]
-    orbits = dirs // OCT
-    part = dirs // tiles
-    part_orbits = orbits // tiles
 
     order, position = orbit_order(directions, mirror)
     own_facets = facet_grid(
         wall_blocks[0], wall_count[0], wall_facet[0], wide * high * deep // BLOCK
     ).astype(jnp.float32)
-    def own_bands(values):
-        return lax.dynamic_slice_in_dim(jnp.pad(values, (0, extra)), group * share, share)
-
-    courant, rates = own_bands(band_courant), own_bands(relax_rate)
-    magnitudes = own_bands(mode_heat_magnitude)
-    pulsations = lax.dynamic_slice_in_dim(
-        jnp.pad(mode_pulsation, (0, extra), constant_values=1.0), group * share, share
-    )
-    reps = lax.dynamic_slice_in_dim(
-        order.reshape(orbits, OCT)[:, OCT - 1], tile * part_orbits, part_orbits
-    )
-    columns = []
-    for axis_num in range(3):
-        unit = jnp.abs(pick(directions[axis_num], reps))
-        columns.extend(beam_coeffs(courant[:, None] * unit[None, :]))
-    columns.append(rates[:, None] * pick(quad_weight, reps)[None, :])
-    columns.append(jnp.broadcast_to(rates[:, None], columns[0].shape))
-    coefs = jnp.stack(columns, axis=-1).reshape(share * part_orbits, len(columns))
-
     home = phonon_heat_density
     if extra:
         home = jnp.pad(home, ((0, 0), (0, extra), (0, 0), (0, 0), (0, 0)))
-    field, source, facets = spread(
-        tiles, groups, share, order, coefs, own_facets.reshape(rows, deep), home
-    )
-    collision_speed_factor = relax_rate * mode_heat_magnitude
-    source = total(tiles, groups, source)
-    kelvin = root_finder_guess(source.reshape(-1), collision_speed_factor, mode_pulsation)
-    bose = magnitudes[:, None, None, None] / jnp.expm1(
-        pulsations[:, None, None, None] / kelvin.reshape((1,) + source.shape)
-    )
-    moved, source = collect(tiles, groups, position, coefs, facets, field, bose, high)
-    kelvin = root_finder_guess(source.reshape(-1), collision_speed_factor, mode_pulsation)
+    scalars = (
+        order,
+        directions,
+        quad_weight,
+        band_courant,
+        relax_rate,
+        mode_heat_magnitude,
+        mode_pulsation,
+    )
+    field, kelvin, facets = spread(
+        tiles, groups, share, scalars, own_facets.reshape(rows, deep), home
+    )
+    moved, kelvin = collect(tiles, groups, position, scalars, facets, field, kelvin, high)
     kelvin = kelvin.reshape(wide, high, deep)
     moved = moved[:, :bands]
     home = mode_heat_magnitude[:, None, None, None] / jnp.expm1(

time: 314 us -> 289 us (0.920)
  other arithmetic: 24.3 us -> 10.6 us
  local copies, waits for them, and re-layouts: 9.22 us -> 2.12 us
  Pallas kernels: 277 us -> 272 us
    pallas_call x1 -> x0, Pallas kernels: 17 us -> none  [total(): pl.pallas_call(functools.partial(total_kernel, tiles, groups), in_specs=[...]
    pallas_call x1, Pallas kernels: 129 us -> 145 us  [spread(): pl.pallas_call(functools.partial(spread_kernel, tiles, groups), in_specs=...]
    min x8 -> x0, other arithmetic: 7.3 us -> none  [root_finder_guess(): jnp.clip(pseudo_kelvin_field - mismatch_error / gradient_guess, 0.5 * pse...]
    reduce_sum x7 -> x0, other arithmetic: 5.2 us -> none  [root_finder_guess(): jnp.sum(collision_speed_factor[:, None] / heat_surplus, axis=0)]
    pallas_call x1, Pallas kernels: 131 us -> 127 us  [collect(): pl.pallas_call(functools.partial(collect_kernel, tiles, groups), in_specs...]
where the time goes in v4:
time: 289 us; the launch traced here: 287 us
  Pallas kernels  272 us (94%)
  other arithmetic  10.6 us (4%)
    pallas_call x1, Pallas kernels, spread(): pl.pallas_call(functools.partial(spread_kernel, tiles, groups), in_specs=...  145 us
    pallas_call x1, Pallas kernels, collect(): pl.pallas_call(functools.partial(collect_kernel, tiles, groups), in_specs...  127 us
    add x1, other arithmetic, on_device(): out = moved + relax_rate[None, :, None, None, None] * (home[None] - moved)  6.28 us

profile of v4, /device:TPU:0, one launch (start us, length us, event | category | flops | bytes accessed | tf_op | source)
XLA Modules:
  0.0 286.5 jit_solution(10520186502716808621)
XLA Ops:
  1.3 0.7 fusion.2
  2.0 0.8 slice_bitcast_fusion
  2.8 0.1 select_reduce_fusion.5
  2.9 0.7 compare_convert_fusion
  3.6 0.2 select_reduce_fusion.4
  3.7 0.2 select_reduce_fusion.3
  4.0 0.2 select_reduce_fusion.2
  4.1 0.5 bitcast_add_fusion.1.position_ref
  4.7 0.6 select_reduce_fusion.1.order_ref
  5.3 0.8 select_reduce_fusion
  6.1 0.6 convert_element_type.12.facet_ref
  6.7 0.0 copy-start.1
  6.7 0.0 copy-start.2
  6.7 0.0 copy-start.3
  6.7 145.2 %shard_map.122 = (f32[4,32,5,8,256]{4,3,2,1,0:T(8,128)}, f32[4,8,256]{2,1,0:T(8,128)}, f32[4,8,256]{2,1,0:T(8,128)}) custom-call(s32[128]{0:T(128)} %select_reduce_fusion.1.order_ref, f32[3,128]{1,0:T(4,128)} %directions_ref.3, f32[128]{0:T(128)} %weight_ref.3, f32[40]{0:T(128)} %courant_ref.3, f32[40]{0:T(128)} %rate_ref.3, f32[40]{0:T(128)} %magnitude_ref.3, ...), custom_call_target="tpu_custom_call" | custom-call | tf_op jit(solution)/shard_map/pallas_call | solution.py:341
  151.9 127.2 %shard_map.123 = (f32[16,40,2,4,256]{4,3,2,1,0:T(4,128)}, f32[8,256]{1,0:T(8,128)}) custom-call(s32[128]{0:T(128)} %bitcast_add_fusion.1.position_ref, s32[128]{0:T(128)} %select_reduce_fusion.1.order_ref, f32[3,128]{1,0:T(4,128)} %directions_ref.3, f32[128]{0:T(128)} %weight_ref.3, f32[40]{0:T(128)} %courant_ref.3, f32[40]{0:T(128)} %rate_ref.3, ...), custom_call_target="tpu_custom_call" | custom-call | tf_op jit(solution)/shard_map/pallas_call | solution.py:526
  279.2 0.7 div.33
  279.9 0.0 copy-done.1
  279.9 0.0 copy-done.2
  279.9 0.0 copy-start
  279.9 0.3 fusion
  280.3 0.0 copy-done.3
  280.3 6.3 %multiply_add_fusion = f32[16,40,2,4,256]{4,3,2,1,0:T(4,128)} fusion(f32[16,40,2,4,256]{4,3,2,1,0:T(4,128)} %get-tuple-element.10, f32[40,2,4,256]{3,2,1,0:T(4,128)S(1)} %fusion, f32[40]{0:T(128)S(1)} %copy-done.3), kind=kLoop, calls=%fused_computation | loop fusion | flops 3932160 | bytes 10813600 | tf_op jit(solution)/shard_map/add | solution.py:610
  286.5 0.0 copy-done
  (7 shorter events, 0.0 us)
Async XLA Ops:
  6.7 273.2 %copy-start.1 = (f32[40]{0:T(128)S(1)}, f32[40]{0:T(128)}, u32[]{:S(2)}) copy-start(f32[40]{0:T(128)} %magnitude_ref.3) | copy-start | bytes 484
  6.7 273.2 %copy-start.2 = (f32[40]{0:T(128)S(1)}, f32[40]{0:T(128)}, u32[]{:S(2)}) copy-start(f32[40]{0:T(128)} %pulsation_ref.3) | copy-start | bytes 484
  6.7 273.5 %copy-start.3 = (f32[40]{0:T(128)S(1)}, f32[40]{0:T(128)}, u32[]{:S(2)}) copy-start(f32[40]{0:T(128)} %rate_ref.3) | copy-start | bytes 484
  279.9 6.6 %copy-start = (f32[2,4,256]{2,1,0:T(4,128)}, f32[2,4,256]{2,1,0:T(4,128)S(1)}, u32[]{:S(2)}) copy-start(f32[2,4,256]{2,1,0:T(4,128)S(1)} %div.33) | copy-start | bytes 24580
